TPU v7x, 32 devices: a whole 2x2x4 slice. The times are simulated.
32 devices in a mesh: date: 16 (over z, y, core), az: 2 (over x).
Axes of the slice: x: 2, y: 2, z: 4, core: 2. Of those that a mesh axis runs over, the one named last changes fastest.
Arguments:
- raw_stack: float32 [2, 128, 32, 1024], P(None, 'date', None, 'az'), may hold values from -6 to 6
- azimuth_filter: float32 [2, 32, 1024], replicated, may hold values from -6 to 6
- start_vectors: float32 [2, 1024, 32, 128], P(None, 'date', 'az'), may hold values from -6 to 6
- window_offsets: int32 [64, 2, 2], P('date', 'az'), may hold values from -1 to 1
Outputs:
- linked: float32 [2, 1024, 32, 128], P(None, 'date', 'az')
All inputs are finite; a program needn't handle non-finite values.
Results may differ from a plain program's by a relative error of at most 0.0003.
Values sent between devices are 32-bit elements; how exact they have to be, the bound alone decides.
A program may use at most 128 MiB of HBM per device.

v0:
```python
import math

import jax
import jax.numpy as jnp
from jax import lax
from jax.sharding import PartitionSpec as P

TILE = 16
WIN = 5
ITERS = 8


def padded(block, sides, width):
    for axis, dim in sides:
        count = lax.axis_size(axis)
        forward = [(i, i + 1) for i in range(count - 1)]
        backward = [(target, source) for source, target in forward]
        low = lax.ppermute(
            lax.slice_in_dim(block, block.shape[dim] - width, None, axis=dim), axis, forward
        )
        high = lax.ppermute(lax.slice_in_dim(block, 0, width, axis=dim), axis, backward)
        block = jnp.concatenate([low, block, high], axis=dim)
    return block


def tables(length):
    index = jnp.arange(length, dtype=jnp.int32)
    phase = index[:, None] * index[None, :] % length
    angle = phase.astype(jnp.float32) * (2.0 * math.pi / length)
    return (jnp.cos(angle), jnp.sin(angle))


def focus(signal, filt):
    cosine, sine = tables(signal.shape[3])
    highest = lax.Precision.HIGHEST

    def forward(field, table):
        return jnp.einsum("dca,ak->dck", field, table, precision=highest)

    def backward(field, table):
        return jnp.einsum("dck,ka->acd", field, table, precision=highest)

    real_in, imag_in = (signal[0], signal[1])
    spec_real = forward(real_in, cosine) + forward(imag_in, sine)
    spec_imag = forward(imag_in, cosine) - forward(real_in, sine)
    filt_real = spec_real * filt[0] - spec_imag * filt[1]
    filt_imag = spec_real * filt[1] + spec_imag * filt[0]
    inverse = 1.0 / signal.shape[3]
    out_real = (backward(filt_real, cosine) - backward(filt_imag, sine)) * inverse
    out_imag = (backward(filt_imag, cosine) + backward(filt_real, sine)) * inverse
    return jnp.stack([out_real, out_imag])


def link(window, start):
    side = start.shape[1]
    real_z, imag_z = (window[0], window[1])
    views = [
        (real_z[a : a + side, b : b + side], imag_z[a : a + side, b : b + side])
        for a in range(WIN)
        for b in range(WIN)
    ]
    power = jnp.zeros_like(start[0])
    for view_real, view_imag in views:
        power = power + view_real * view_real + view_imag * view_imag
    scale = 1.0 / jnp.sqrt(power + 1e-06)
    vec_real, vec_imag = (start[0], start[1])
    for step in range(ITERS):
        wgt_real, wgt_imag = (vec_real * scale, vec_imag * scale)
        acc_real = jnp.zeros_like(vec_real)
        acc_imag = jnp.zeros_like(vec_imag)
        for view_real, view_imag in views:
            proj_real = jnp.sum(view_real * wgt_real + view_imag * wgt_imag, axis=-1, keepdims=True)
            proj_imag = jnp.sum(view_real * wgt_imag - view_imag * wgt_real, axis=-1, keepdims=True)
            acc_real = acc_real + view_real * proj_real - view_imag * proj_imag
            acc_imag = acc_imag + view_real * proj_imag + view_imag * proj_real
        gam_real, gam_imag = (acc_real * scale, acc_imag * scale)
        length = jnp.sqrt(
            jnp.sum(gam_real * gam_real + gam_imag * gam_imag, axis=-1, keepdims=True) + 1e-06
        )
        vec_real, vec_imag = (gam_real / length, gam_imag / length)
    return jnp.stack([vec_real, vec_imag])


def shards(raw_stack, azimuth_filter, start_vectors, window_offsets):
    rim = WIN // 2 + 1
    az_parts = lax.axis_size("az")
    date_parts = lax.axis_size("date")
    az_place = lax.axis_index("az")
    bins = raw_stack.shape[2] // az_parts
    lines = raw_stack.shape[3] * az_parts // date_parts
    turned = lax.all_to_all(raw_stack, "az", split_axis=2, concat_axis=3, tiled=True)
    filt_part = lax.dynamic_slice_in_dim(azimuth_filter, az_place * bins, bins, 1)
    focused = focus(turned, filt_part)
    regrouped = lax.all_to_all(focused, "date", split_axis=1, concat_axis=3, tiled=True)
    window_all = padded(regrouped, (("date", 1), ("az", 2)), rim)
    rows_tiles = lines // TILE
    cols_tiles = bins // TILE
    dates = window_all.shape[3]
    span = TILE + WIN - 1
    numbers = jnp.arange(rows_tiles * cols_tiles, dtype=jnp.int32)
    tile_rows = numbers // cols_tiles
    tile_cols = numbers % cols_tiles
    shifts = window_offsets.reshape(rows_tiles * cols_tiles, 2)

    def cut_window(tile_row, tile_col, shift):
        zero = jnp.zeros((), jnp.int32)
        first_row = tile_row * TILE + 1 + shift[0]
        first_col = tile_col * TILE + 1 + shift[1]
        return lax.dynamic_slice(
            window_all, (zero, first_row, first_col, zero), (2, span, span, dates)
        )

    windows = jax.vmap(cut_window)(tile_rows, tile_cols, shifts)
    starts = start_vectors.reshape(2, rows_tiles, TILE, cols_tiles, TILE, dates)
    starts = jnp.transpose(starts, (1, 3, 0, 2, 4, 5)).reshape(
        rows_tiles * cols_tiles, 2, TILE, TILE, dates
    )
    results = jax.vmap(link)(windows, starts)
    results = results.reshape(rows_tiles, cols_tiles, 2, TILE, TILE, dates)
    results = jnp.transpose(results, (2, 0, 3, 1, 4, 5))
    return results.reshape(2, lines, bins, dates)


def solution(mesh):
    placed = (P(None, "date", None, "az"), P(), P(None, "date", "az", None), P("date", "az", None))
    return jax.shard_map(
        shards, mesh=mesh, in_specs=placed, out_specs=P(None, "date", "az", None), check_vma=False
    )
```

profile of v0, /device:TPU:9, one launch (start us, length us, event | category | flops | bytes accessed | tf_op | source)
XLA Modules:
  0.0 522.7 jit_solution(5264643630380432611)
XLA Ops:
  6.5 12.9 %all-to-all-done = f32[2,8,32,512]{3,1,0,2:T(8,128)S(1)} async-done(((f32[2,8,32,512]{3,1,0,2:T(8,128)}), f32[2,8,32,512]{3,1,0,2:T(8,128)S(1)}, u32[]{:S(2)}, u32[]{:S(2)}) %all-to-all-start) | async-done | bytes 1048608 | tf_op jit(solution)/shard_map/all_to_all | solution.py:91
  21.6 18.7 %fusion.7 = f32[1024,8,16]{0,2,1:T(8,128)S(1)} fusion(f32[8,16,1024]{2,1,0:T(8,128)S(1)} %squeeze.20), kind=kOutput, calls=%fused_computation.11 | convolution fusion | flops 1625292800 | bytes 1048576 | tf_op jit(solution)/shard_map/dca,ak->dck/dot_general | solution.py:38
  40.3 18.7 %fusion.9 = f32[1024,8,16]{0,2,1:T(8,128)S(1)} fusion(f32[8,16,1024]{2,1,0:T(8,128)S(1)} %squeeze.21), kind=kOutput, calls=%fused_computation.13 | convolution fusion | flops 1625292800 | bytes 1048576 | tf_op jit(solution)/shard_map/dca,ak->dck/dot_general | solution.py:38
  59.1 18.7 %fusion.41 = f32[8,16,1024]{2,1,0:T(8,128)S(1)} fusion(f32[1024,8,16]{0,2,1:T(8,128)S(1)} %fusion.7, f32[8,16,1024]{2,1,0:T(8,128)S(1)} %squeeze.21), kind=kOutput, calls=%fused_computation.32 | convolution fusion | flops 1625423872 | bytes 1572864 | tf_op jit(solution)/shard_map/dca,ak->dck/dot_general | solution.py:38
  77.8 18.5 %fusion.35 = f32[8,16,1024]{2,1,0:T(8,128)S(1)} fusion(f32[1024,8,16]{0,2,1:T(8,128)S(1)} %fusion.9, f32[8,16,1024]{2,1,0:T(8,128)S(1)} %squeeze.20), kind=kOutput, calls=%fused_computation.30 | convolution fusion | flops 1625423872 | bytes 1572864 | tf_op jit(solution)/shard_map/dca,ak->dck/dot_general | solution.py:38
  96.3 19.3 %fusion.3 = f32[1024,8,16]{0,2,1:T(8,128)S(1)} fusion(f32[8,16,1024]{2,1,0:T(8,128)S(1)} %fusion.41, f32[8,16,1024]{2,1,0:T(8,128)S(1)} %fusion.35, f32[16,1024]{1,0:T(8,128)S(1)} %get-tuple-element.841, f32[16,1024]{1,0:T(8,128)S(1)} %get-tuple-element.840), kind=kOutput, calls=%fused_computation.7 | convolution fusion | flops 1625686016 | bytes 1703936 | tf_op jit(solution)/shard_map/dck,ka->acd/dot_general | solution.py:41
  115.6 18.9 %fusion.5 = f32[1024,8,16]{0,2,1:T(8,128)S(1)} fusion(f32[8,16,1024]{2,1,0:T(8,128)S(1)} %fusion.41, f32[8,16,1024]{2,1,0:T(8,128)S(1)} %fusion.35, f32[16,1024]{1,0:T(8,128)S(1)} %get-tuple-element.841, f32[16,1024]{1,0:T(8,128)S(1)} %get-tuple-element.840), kind=kOutput, calls=%fused_computation.9 | convolution fusion | flops 1625686016 | bytes 1703936 | tf_op jit(solution)/shard_map/dck,ka->acd/dot_general | solution.py:41
  134.5 18.9 %fusion.53 = f32[1,1024,16,8]{1,2,3,0:T(8,128)S(1)} fusion(f32[1024,8,16]{0,2,1:T(8,128)S(1)} %fusion.3, f32[8,16,1024]{2,1,0:T(8,128)S(1)} %fusion.41, f32[8,16,1024]{2,1,0:T(8,128)S(1)} %fusion.35, f32[16,1024]{1,0:T(8,128)S(1)} %get-tuple-element.841, f32[16,1024]{1,0:T(8,128)S(1)} %get-tuple-element.840), kind=kOutput, calls=%fused_computation.36 | convolution fusion | flops 1625948160 | bytes 2228224 | tf_op jit(solution)/shard_map/dck,ka->acd/dot_general | solution.py:41
  153.4 18.8 %fusion.59 = f32[1,1024,16,8]{1,2,3,0:T(8,128)S(1)} fusion(f32[1024,8,16]{0,2,1:T(8,128)S(1)} %fusion.5, f32[8,16,1024]{2,1,0:T(8,128)S(1)} %fusion.41, f32[8,16,1024]{2,1,0:T(8,128)S(1)} %fusion.35, f32[16,1024]{1,0:T(8,128)S(1)} %get-tuple-element.841, f32[16,1024]{1,0:T(8,128)S(1)} %get-tuple-element.840), kind=kOutput, calls=%fused_computation.38 | convolution fusion | flops 1625948160 | bytes 2228224 | tf_op jit(solution)/shard_map/dck,ka->acd/dot_general | solution.py:41
  172.3 6.2 %copy.68 = f32[2,1024,16,8]{2,3,0,1:T(8,128)} copy(f32[2,1024,16,8]{1,2,3,0:T(8,128)S(1)} %pad_maximum_fusion.1) | data formatting | bytes 2097152 | tf_op jit(solution)/shard_map/stack | solution.py:51
  178.4 6.3 %reshape.490 = f32[16,1,16384]{2,1,0:T(1,128)S(1)} reshape(f32[1024,2,8,16]{3,2,1,0:T(8,128)} %bitcast.102) | data formatting | bytes 2097152
  184.8 32.7 %all_to_all.33 = f32[16,1,16384]{2,1,0:T(1,128)S(1)} all-to-all(f32[16,1,16384]{2,1,0:T(1,128)S(1)} %reshape.490), channel_id=1, replica_groups=mesh['date'=16,'az'=2] {'date'}, dimensions={0} | all-to-all | bytes 2097152 | tf_op jit(solution)/shard_map/all_to_all | solution.py:94
  221.1 4.8 reshape.491
  225.9 5.8 %copy.69 = f32[2,16,64,16,8]{2,4,1,3,0:T(8,128)S(1)} copy(f32[2,16,64,16,8]{3,4,0,2,1:T(8,128)} %bitcast.101) | data formatting | bytes 2097152 | tf_op jit(solution)/shard_map/all_to_all | solution.py:94
  282.0 6.0 %add_reduce_fusion.205 = (f32[4,16,16]{2,1,0:T(8,128)S(1)}, f32[4,16,16]{2,1,0:T(8,128)S(1)}, f32[4,16,16]{2,1,0:T(8,128)S(1)}, f32[4,16,16]{2,1,0:T(8,128)S(1)}...) fusion(f32[4,16,16,128]{3,2,1,0:T(8,128)S(1)} %get-tuple-elemen, ...), kind=kLoop, calls=%fused_computation.483 | loop fusion | flops 8372224 | bytes 9502720 | tf_op jit(solution)/shard_map/vmap()/reduce_sum | solution.py:72
  294.7 13.4 %add_reduce_fusion.182 = (f32[4,16,16]{2,1,0:T(8,128)S(1)}, f32[4,16,16,128]{3,2,1,0:T(8,128)S(1)}, f32[4,16,16,128]{3,2,1,0:T(8,128)S(1)}) fusion(f32[4,16,16,128]{3,2,1,0:T(8,128)S(1)} %add_rsqrt_fusion, f32[4,16,16]{2,1,0:T(8,128)S(1)} %get-tuple-element.699, f32[4,16,16,128]{3,0,2,1:T(4,128)S(1)} %get-tuple-element.833, ...), kind=kLoop, calls=%fused_computation.435 | loop fusion | flops 26737664 | bytes 27996160 | tf_op jit(solution)/shard_map/vmap()/reduce_sum | solution.py:78
  314.6 4.9 add_reduce_fusion.179
  323.6 13.8 %add_reduce_fusion.156 = (f32[4,16,16]{2,1,0:T(8,128)S(1)}, f32[4,16,16,128]{3,2,1,0:T(8,128)S(1)}, f32[4,16,16,128]{3,2,1,0:T(8,128)S(1)}) fusion(f32[4,16,16,128]{3,2,1,0:T(8,128)S(1)} %add_rsqrt_fusion, f32[4,16,16]{2,1,0:T(8,128)S(1)} %get-tuple-element.657, f32[4,16,16,128]{3,0,2,1:T(4,128)S(1)} %get-tuple-element.833, ...), kind=kLoop, calls=%fused_computation.380 | loop fusion | flops 26737664 | bytes 27996160 | tf_op jit(solution)/shard_map/vmap()/reduce_sum | solution.py:78
  343.4 4.9 add_reduce_fusion.153
  352.4 13.6 %add_reduce_fusion.130 = (f32[4,16,16]{2,1,0:T(8,128)S(1)}, f32[4,16,16,128]{3,2,1,0:T(8,128)S(1)}, f32[4,16,16,128]{3,2,1,0:T(8,128)S(1)}) fusion(f32[4,16,16,128]{3,2,1,0:T(8,128)S(1)} %add_rsqrt_fusion, f32[4,16,16]{2,1,0:T(8,128)S(1)} %get-tuple-element.615, f32[4,16,16,128]{3,0,2,1:T(4,128)S(1)} %get-tuple-element.833, ...), kind=kLoop, calls=%fused_computation.325 | loop fusion | flops 26737664 | bytes 27996160 | tf_op jit(solution)/shard_map/vmap()/reduce_sum | solution.py:78
  371.9 4.9 add_reduce_fusion.127
  381.3 13.6 %add_reduce_fusion.104 = (f32[4,16,16]{2,1,0:T(8,128)S(1)}, f32[4,16,16,128]{3,2,1,0:T(8,128)S(1)}, f32[4,16,16,128]{3,2,1,0:T(8,128)S(1)}) fusion(f32[4,16,16,128]{3,2,1,0:T(8,128)S(1)} %add_rsqrt_fusion, f32[4,16,16]{2,1,0:T(8,128)S(1)} %get-tuple-element.573, f32[4,16,16,128]{3,0,2,1:T(4,128)S(1)} %get-tuple-element.833, ...), kind=kLoop, calls=%fused_computation.270 | loop fusion | flops 26737664 | bytes 27996160 | tf_op jit(solution)/shard_map/vmap()/reduce_sum | solution.py:78
  400.9 4.9 add_reduce_fusion.101
  409.9 13.6 %add_reduce_fusion.78 = (f32[4,16,16]{2,1,0:T(8,128)S(1)}, f32[4,16,16,128]{3,2,1,0:T(8,128)S(1)}, f32[4,16,16,128]{3,2,1,0:T(8,128)S(1)}) fusion(f32[4,16,16,128]{3,2,1,0:T(8,128)S(1)} %add_rsqrt_fusion, f32[4,16,16]{2,1,0:T(8,128)S(1)} %get-tuple-element.531, f32[4,16,16,128]{3,0,2,1:T(4,128)S(1)} %get-tuple-element.833, ...), kind=kLoop, calls=%fused_computation.215 | loop fusion | flops 26737664 | bytes 27996160 | tf_op jit(solution)/shard_map/vmap()/reduce_sum | solution.py:78
  429.5 5.1 add_reduce_fusion.75
  438.7 13.6 %add_reduce_fusion.52 = (f32[4,16,16]{2,1,0:T(8,128)S(1)}, f32[4,16,16,128]{3,2,1,0:T(8,128)S(1)}, f32[4,16,16,128]{3,2,1,0:T(8,128)S(1)}) fusion(f32[4,16,16,128]{3,2,1,0:T(8,128)S(1)} %add_rsqrt_fusion, f32[4,16,16]{2,1,0:T(8,128)S(1)} %get-tuple-element.489, f32[4,16,16,128]{3,0,2,1:T(4,128)S(1)} %get-tuple-element.833, ...), kind=kLoop, calls=%fused_computation.160 | loop fusion | flops 26737664 | bytes 27996160 | tf_op jit(solution)/shard_map/vmap()/reduce_sum | solution.py:78
  458.2 4.9 add_reduce_fusion.49
  467.2 13.6 %add_reduce_fusion.26 = (f32[4,16,16]{2,1,0:T(8,128)S(1)}, f32[4,16,16,128]{3,2,1,0:T(8,128)S(1)}, f32[4,16,16,128]{3,2,1,0:T(8,128)S(1)}) fusion(f32[4,16,16,128]{3,2,1,0:T(8,128)S(1)} %add_rsqrt_fusion, f32[4,16,16]{2,1,0:T(8,128)S(1)} %get-tuple-element.447, f32[4,16,16,128]{3,0,2,1:T(4,128)S(1)} %get-tuple-element.833, ...), kind=kLoop, calls=%fused_computation.105 | loop fusion | flops 26737664 | bytes 27996160 | tf_op jit(solution)/shard_map/vmap()/reduce_sum | solution.py:78
  482.8 5.6 %add_reduce_fusion.23 = (f32[4,16,16]{2,1,0:T(8,128)S(1)}, f32[4,16,16]{2,1,0:T(8,128)}, f32[4,16,16]{2,1,0:T(8,128)}, f32[4,16,16]{2,1,0:T(8,128)}, f32[4,16,16...) fusion(f32[4,16,16,128]{3,2,1,0:T(8,128)S(1)} %get-tuple-elemen, ...), kind=kLoop, calls=%fused_computation.98 | loop fusion | flops 8372224 | bytes 9502720 | tf_op jit(solution)/shard_map/vmap()/reduce_sum | solution.py:72
  488.4 5.2 %add_reduce_fusion.24 = (f32[4,16,16]{2,1,0:T(8,128)}, f32[4,16,16]{2,1,0:T(8,128)}, f32[4,16,16]{2,1,0:T(8,128)}, f32[4,16,16]{2,1,0:T(8,128)}, f32[4,16,16]{2,...) fusion(f32[4,16,16,128]{3,2,1,0:T(8,128)S(1)} %get-tuple-elemen, ...), kind=kLoop, calls=%fused_computation.100 | loop fusion | flops 8372224 | bytes 9502720 | tf_op jit(solution)/shard_map/vmap()/reduce_sum | solution.py:72
  493.8 5.0 add_reduce_fusion.25
  499.1 20.3 %add_reduce_fusion = (f32[4,16,16]{2,1,0:T(8,128)}, f32[4,16,16,128]{3,2,1,0:T(8,128)S(1)}, f32[4,16,16,128]{3,2,1,0:T(8,128)}) fusion(f32[4,16,16,128]{3,2,1,0:T(8,128)S(1)} %add_rsqrt_fusion, f32[4,16,16]{2,1,0:T(8,128)} %get-tuple-element.405, f32[4,16,16,128]{3,0,2,1:T(4,128)S(1)} %get-tuple-element.833, f32[4,16,16]{2,1,0:T(8,128)} %get-tuple-element.406, ...), kind=kLoop, calls=%fused_computation.50 | loop fusion | flops 26737664 | bytes 27996160 | tf_op jit(solution)/shard_map/vmap()/reduce_sum | solution.py:78
  (265 shorter events, 134.2 us)
Async XLA Ops:
  2.9 16.6 %all-to-all-start = ((f32[2,8,32,512]{3,1,0,2:T(8,128)}), f32[2,8,32,512]{3,1,0,2:T(8,128)S(1)}, u32[]{:S(2)}, u32[]{:S(2)}) async-start(f32[2,8,32,512]{3,1,0,2:T(8,128)} %copy.66), calls=%async_computation | async-start | bytes 2097152 | tf_op jit(solution)/shard_map/all_to_all | solution.py:91
  231.7 12.9 %copy-start.86 = (s32[4,1,2]{0,2,1:T(2,128)S(1)}, s32[4,1,2]{0,2,1:T(2,128)}, u32[]{:S(2)}) copy-start(s32[4,1,2]{0,2,1:T(2,128)} %param.7) | copy-start | bytes 100
  233.1 4.6 collective-permute-start
  235.7 5.4 %collective-permute-start.1 = (f32[2,3,16,128]{3,0,2,1:T(2,128)S(1)}, f32[2,3,16,128]{3,0,2,1:T(2,128)S(1)}, u32[]{:S(2)}, u32[]{:S(2)}) collective-permute-start(f32[2,3,16,128]{3,0,2,1:T(2,128)S(1)} %get-tuple-element.786), channel_id=1, source_target_pairs={{2,0},{4,2},{6,4},{8,6},{10,8},{12,10},{14,12},{16,14},{18,16},{20... | collective-permute-start | bytes 147464 | tf_op jit(solution)/shard_map/ppermute | solution.py:21
  241.4 6.6 %collective-permute-start.2 = (f32[2,70,3,128]{3,0,2,1:T(2,128)S(1)}, f32[2,70,3,128]{3,0,2,1:T(2,128)S(1)}, u32[]{:S(2)}, u32[]{:S(2)}) collective-permute-start(f32[2,70,3,128]{3,0,2,1:T(2,128)S(1)} %get-tuple-element.783), channel_id=1, source_target_pairs={{0,1},{2,3},{4,5},{6,7},{8,9},{10,11},{12,13},{14,15},{16,17},{18,... | collective-permute-start | bytes 645128 | tf_op jit(solution)/shard_map/ppermute | solution.py:18
  243.3 8.5 %collective-permute-start.3 = (f32[2,70,3,128]{3,0,2,1:T(2,128)S(1)}, f32[2,70,3,128]{3,0,2,1:T(2,128)S(1)}, u32[]{:S(2)}, u32[]{:S(2)}) collective-permute-start(f32[2,70,3,128]{3,0,2,1:T(2,128)S(1)} %get-tuple-element.784), channel_id=1, source_target_pairs={{1,0},{3,2},{5,4},{7,6},{9,8},{11,10},{13,12},{15,14},{17,16},{19,... | collective-permute-start | bytes 645128 | tf_op jit(solution)/shard_map/ppermute | solution.py:21
  262.1 25.9 %copy-start.44 = (f32[4,16,16,128]{3,0,2,1:T(4,128)}, f32[4,16,16,128]{3,0,2,1:T(4,128)S(1)}, u32[]{:S(2)}) copy-start(f32[4,16,16,128]{3,0,2,1:T(4,128)S(1)} %get-tuple-element.832) | copy-start | bytes 1572868
  262.1 28.9 %copy-start.45 = (f32[4,16,16,128]{3,0,2,1:T(4,128)}, f32[4,16,16,128]{3,0,2,1:T(4,128)S(1)}, u32[]{:S(2)}) copy-start(f32[4,16,16,128]{3,0,2,1:T(4,128)S(1)} %get-tuple-element.831) | copy-start | bytes 1572868
  264.5 26.5 %copy-start.47 = (f32[4,16,16,128]{3,0,2,1:T(4,128)}, f32[4,16,16,128]{3,0,2,1:T(4,128)S(1)}, u32[]{:S(2)}) copy-start(f32[4,16,16,128]{3,0,2,1:T(4,128)S(1)} %get-tuple-element.789) | copy-start | bytes 1572868
  264.5 26.5 %copy-start.49 = (f32[4,16,16,128]{3,0,2,1:T(4,128)}, f32[4,16,16,128]{3,0,2,1:T(4,128)S(1)}, u32[]{:S(2)}) copy-start(f32[4,16,16,128]{3,0,2,1:T(4,128)S(1)} %get-tuple-element.799) | copy-start | bytes 1572868
  264.6 26.5 %copy-start.51 = (f32[4,16,16,128]{3,0,2,1:T(4,128)}, f32[4,16,16,128]{3,0,2,1:T(4,128)S(1)}, u32[]{:S(2)}) copy-start(f32[4,16,16,128]{3,0,2,1:T(4,128)S(1)} %get-tuple-element.800) | copy-start | bytes 1572868
  264.6 26.5 %copy-start.53 = (f32[4,16,16,128]{3,0,2,1:T(4,128)}, f32[4,16,16,128]{3,0,2,1:T(4,128)S(1)}, u32[]{:S(2)}) copy-start(f32[4,16,16,128]{3,0,2,1:T(4,128)S(1)} %get-tuple-element.801) | copy-start | bytes 1572868
  265.0 23.0 %copy-start.46 = (f32[4,16,16,128]{3,0,2,1:T(4,128)}, f32[4,16,16,128]{3,0,2,1:T(4,128)S(1)}, u32[]{:S(2)}) copy-start(f32[4,16,16,128]{3,0,2,1:T(4,128)S(1)} %get-tuple-element.838) | copy-start | bytes 1572868
  265.0 26.0 %copy-start.55 = (f32[4,16,16,128]{3,0,2,1:T(4,128)}, f32[4,16,16,128]{3,0,2,1:T(4,128)S(1)}, u32[]{:S(2)}) copy-start(f32[4,16,16,128]{3,0,2,1:T(4,128)S(1)} %get-tuple-element.837) | copy-start | bytes 1572868
  268.6 8.1 %copy-start = (f32[4,16,16,128]{3,2,1,0:T(8,128)}, f32[4,16,16,128]{3,2,1,0:T(8,128)S(1)}, u32[]{:S(2)}) copy-start(f32[4,16,16,128]{3,2,1,0:T(8,128)S(1)} %copy.134) | copy-start | bytes 1572868
  268.7 8.0 %copy-start.2 = (f32[4,16,16,128]{3,2,1,0:T(8,128)}, f32[4,16,16,128]{3,2,1,0:T(8,128)S(1)}, u32[]{:S(2)}) copy-start(f32[4,16,16,128]{3,2,1,0:T(8,128)S(1)} %copy.132) | copy-start | bytes 1572868
  268.7 8.0 %copy-start.4 = (f32[4,16,16,128]{3,2,1,0:T(8,128)}, f32[4,16,16,128]{3,2,1,0:T(8,128)S(1)}, u32[]{:S(2)}) copy-start(f32[4,16,16,128]{3,2,1,0:T(8,128)S(1)} %copy.130) | copy-start | bytes 1572868
  268.8 7.9 %copy-start.6 = (f32[4,16,16,128]{3,2,1,0:T(8,128)}, f32[4,16,16,128]{3,2,1,0:T(8,128)S(1)}, u32[]{:S(2)}) copy-start(f32[4,16,16,128]{3,2,1,0:T(8,128)S(1)} %copy.128) | copy-start | bytes 1572868
  268.8 7.9 %copy-start.8 = (f32[4,16,16,128]{3,2,1,0:T(8,128)}, f32[4,16,16,128]{3,2,1,0:T(8,128)S(1)}, u32[]{:S(2)}) copy-start(f32[4,16,16,128]{3,2,1,0:T(8,128)S(1)} %copy.126) | copy-start | bytes 1572868
  268.9 7.8 %copy-start.10 = (f32[4,16,16,128]{3,2,1,0:T(8,128)}, f32[4,16,16,128]{3,2,1,0:T(8,128)S(1)}, u32[]{:S(2)}) copy-start(f32[4,16,16,128]{3,2,1,0:T(8,128)S(1)} %copy.133) | copy-start | bytes 1572868
  269.0 7.8 %copy-start.12 = (f32[4,16,16,128]{3,2,1,0:T(8,128)}, f32[4,16,16,128]{3,2,1,0:T(8,128)S(1)}, u32[]{:S(2)}) copy-start(f32[4,16,16,128]{3,2,1,0:T(8,128)S(1)} %copy.131) | copy-start | bytes 1572868
  269.0 7.7 %copy-start.14 = (f32[4,16,16,128]{3,2,1,0:T(8,128)}, f32[4,16,16,128]{3,2,1,0:T(8,128)S(1)}, u32[]{:S(2)}) copy-start(f32[4,16,16,128]{3,2,1,0:T(8,128)S(1)} %copy.129) | copy-start | bytes 1572868
  269.1 7.7 %copy-start.16 = (f32[4,16,16,128]{3,2,1,0:T(8,128)}, f32[4,16,16,128]{3,2,1,0:T(8,128)S(1)}, u32[]{:S(2)}) copy-start(f32[4,16,16,128]{3,2,1,0:T(8,128)S(1)} %copy.127) | copy-start | bytes 1572868
  269.2 7.6 %copy-start.18 = (f32[4,16,16,128]{3,2,1,0:T(8,128)}, f32[4,16,16,128]{3,2,1,0:T(8,128)S(1)}, u32[]{:S(2)}) copy-start(f32[4,16,16,128]{3,2,1,0:T(8,128)S(1)} %copy.125) | copy-start | bytes 1572868
  269.4 7.4 %copy-start.20 = (f32[4,16,16,128]{3,2,1,0:T(8,128)}, f32[4,16,16,128]{3,2,1,0:T(8,128)S(1)}, u32[]{:S(2)}) copy-start(f32[4,16,16,128]{3,2,1,0:T(8,128)S(1)} %copy.145) | copy-start | bytes 1572868
  269.4 7.4 %copy-start.22 = (f32[4,16,16,128]{3,2,1,0:T(8,128)}, f32[4,16,16,128]{3,2,1,0:T(8,128)S(1)}, u32[]{:S(2)}) copy-start(f32[4,16,16,128]{3,2,1,0:T(8,128)S(1)} %copy.143) | copy-start | bytes 1572868
  269.9 10.0 %copy-start.32 = (f32[4,16,16,128]{3,2,1,0:T(8,128)}, f32[4,16,16,128]{3,2,1,0:T(8,128)S(1)}, u32[]{:S(2)}) copy-start(f32[4,16,16,128]{3,2,1,0:T(8,128)S(1)} %copy.146) | copy-start | bytes 1572868
  271.4 8.6 %copy-start.34 = (f32[4,16,16,128]{3,2,1,0:T(8,128)}, f32[4,16,16,128]{3,2,1,0:T(8,128)S(1)}, u32[]{:S(2)}) copy-start(f32[4,16,16,128]{3,2,1,0:T(8,128)S(1)} %copy.144) | copy-start | bytes 1572868
  488.4 10.4 %copy-start.39 = (f32[4,16,16,128]{3,2,1,0:T(8,128)S(1)}, f32[4,16,16,128]{3,2,1,0:T(8,128)}, u32[]{:S(2)}) copy-start(f32[4,16,16,128]{3,2,1,0:T(8,128)} %copy-done.38) | copy-start | bytes 1572868
  488.4 10.4 %copy-start.41 = (f32[4,16,16,128]{3,2,1,0:T(8,128)S(1)}, f32[4,16,16,128]{3,2,1,0:T(8,128)}, u32[]{:S(2)}) copy-start(f32[4,16,16,128]{3,2,1,0:T(8,128)} %copy-done.40) | copy-start | bytes 1572868
  488.4 10.4 %copy-start.43 = (f32[4,16,16,128]{3,2,1,0:T(8,128)S(1)}, f32[4,16,16,128]{3,2,1,0:T(8,128)}, u32[]{:S(2)}) copy-start(f32[4,16,16,128]{3,2,1,0:T(8,128)} %copy-done.42) | copy-start | bytes 1572868
  488.4 10.4 %copy-start.84 = (f32[4,16,16,128]{3,2,1,0:T(8,128)S(1)}, f32[4,16,16,128]{3,2,1,0:T(8,128)}, u32[]{:S(2)}) copy-start(f32[4,16,16,128]{3,2,1,0:T(8,128)} %get-tuple-element.839) | copy-start | bytes 1572868
  (60 other events, 273.7 us)
where the time goes:
time: 533 us; the launch traced here: 523 us
  other arithmetic  250 us (47%)
  matrix products  151 us (28%)
  local copies, waits for them, and re-layouts  52 us (10%)
  blocking collectives  32.7 us (6%)
  waiting for transfers between devices  23.6 us (4%)
  starting transfers between devices  11.4 us (2%)
    reduce_sum x32, other arithmetic, link(): jnp.sum(view_real * wgt_real + view_imag * wgt_imag, axis=-1, keepdims=True)  122 us
    reduce_sum x8, other arithmetic, link(): jnp.sum(gam_real * gam_real + gam_imag * gam_imag, axis=-1, keepdims=True)  116 us
    dot_general x4, matrix products, backward(): return jnp.einsum('dck,ka->acd', field, table, precision=highest)  75.9 us
    dot_general x4, matrix products, forward(): return jnp.einsum('dca,ak->dck', field, table, precision=highest)  74.7 us
    all_to_all x1, blocking collectives, shards(): lax.all_to_all(focused, 'date', split_axis=1, concat_axis=3, tiled=True)  32.7 us
    unnamed x205, local copies, waits for them, and re-layouts  21.9 us
    all_to_all x1, waiting for transfers between devices, shards(): lax.all_to_all(raw_stack, 'az', split_axis=2, concat_axis=3, tiled=True)  12.9 us
  transfers between devices with their start and end apart: 5, of which 4 were waited for; matrix products, arithmetic and copies ran while one was open for 0% of the time, Pallas kernels for 0%

commit v1 on v0

v1 whole, which is shorter than its diff:
```python
import functools
import math

import jax
import jax.numpy as jnp
import numpy as np
from jax import lax
from jax.experimental import pallas as pl
from jax.experimental.pallas import tpu as pltpu
from jax.sharding import PartitionSpec as P

TILE = 16
WIN = 5
ITERS = 8
RIM = WIN // 2 + 1
HALF = TILE // 2
SPAN_ROWS = HALF + WIN - 1
SPAN_COLS = TILE + WIN - 1
PIXELS = HALF * TILE
USED = SPAN_ROWS * SPAN_COLS
SLOTS = 256
LANES = 128


def parts_of(value):
    high = value.astype(jnp.bfloat16)
    return high, (value - high.astype(jnp.float32)).astype(jnp.bfloat16)


def padded(block, sides, width):
    for axis, dim in sides:
        count = lax.axis_size(axis)
        forward = [(i, i + 1) for i in range(count - 1)]
        backward = [(target, source) for source, target in forward]
        low = lax.ppermute(
            lax.slice_in_dim(block, block.shape[dim] - width, None, axis=dim), axis, forward
        )
        high = lax.ppermute(lax.slice_in_dim(block, 0, width, axis=dim), axis, backward)
        block = jnp.concatenate([low, block, high], axis=dim)
    return block


def butterflies(values, sign):
    count = len(values)
    if count == 1:
        return values
    even = butterflies(values[0::2], sign)
    odd = butterflies(values[1::2], sign)
    low, high = [], []
    for k in range(count // 2):
        (er, ei), (dr, di) = even[k], odd[k]
        if k == 0:
            tr, ti = dr, di
        elif 4 * k == count:
            tr, ti = (-di, dr) if sign > 0 else (di, -dr)
        else:
            c = math.cos(2 * math.pi * k / count)
            s = sign * math.sin(2 * math.pi * k / count)
            tr, ti = dr * c - di * s, dr * s + di * c
        low.append((er + tr, ei + ti))
        high.append((er - tr, ei - ti))
    return low + high


def focus_tables(length):
    radix = length // LANES
    a = np.arange(LANES)
    angle = 2 * np.pi * (np.outer(a, a) % LANES) / LANES
    c, s = np.cos(angle), np.sin(angle)
    forward = np.block([[c, -s], [s, c]])
    backward = np.block([[c, s], [-s, c]])

    def stacked(table):
        high = table.astype(jnp.bfloat16)
        low = (table - high.astype(np.float64)).astype(jnp.bfloat16)
        return np.concatenate([high, high, low], axis=0)

    turn = 2 * np.pi * np.outer(np.arange(radix), a) / length
    twist = np.stack([np.cos(turn), np.sin(turn)]).astype(np.float32)
    return stacked(forward), stacked(backward), twist


def focus_kernel(lines, x_ref, f_ref, fwd_ref, bwd_ref, tw_ref, o_ref):
    rows, length = x_ref.shape[2], x_ref.shape[3]
    radix = length // LANES

    def product(value, table_ref):
        high, low = parts_of(value)
        return jnp.dot(
            jnp.concatenate([high, low, high], axis=1),
            table_ref[...],
            preferred_element_type=jnp.float32,
        )

    cols = [slice(b * LANES, (b + 1) * LANES) for b in range(radix)]
    field = [(x_ref[0, 0, :, c], x_ref[1, 0, :, c]) for c in cols]
    stack = []
    for k, (re, im) in enumerate(butterflies(field, -1)):
        c, s = tw_ref[0, k : k + 1, :], tw_ref[1, k : k + 1, :]
        stack.append(jnp.concatenate([re * c + im * s, im * c - re * s], axis=1))
    spec = product(jnp.concatenate(stack, axis=0), fwd_ref)
    sr, si = spec[:, :LANES], spec[:, LANES:]
    fr = f_ref[0].reshape(radix * rows, LANES)
    fi = f_ref[1].reshape(radix * rows, LANES)
    back = product(jnp.concatenate([sr * fr - si * fi, sr * fi + si * fr], axis=1), bwd_ref)
    inverse = 1.0 / length
    field = []
    for k in range(radix):
        c, s = tw_ref[0, k : k + 1, :] * inverse, tw_ref[1, k : k + 1, :] * inverse
        re = back[k * rows : (k + 1) * rows, :LANES]
        im = back[k * rows : (k + 1) * rows, LANES:]
        field.append((re * c - im * s, im * c + re * s))
    field = butterflies(field, 1)
    for block in range(length // lines):
        b, low = block * lines // LANES, block * lines % LANES
        re, im = field[b]
        o_ref[block, 0] = jnp.concatenate(
            [re[:, low : low + lines], im[:, low : low + lines]], axis=1
        )


def focus(signal, filt, lines):
    _, dates, bins, length = signal.shape
    radix = length // LANES
    forward, backward, twist = focus_tables(length)
    filt = filt.reshape(2, bins, LANES, radix).transpose(0, 3, 1, 2)
    blocks = length // lines
    return pl.pallas_call(
        functools.partial(focus_kernel, lines),
        grid=(dates,),
        in_specs=[
            pl.BlockSpec((2, 1, bins, length), lambda d: (0, d, 0, 0)),
            pl.BlockSpec(filt.shape, lambda d: (0, 0, 0, 0)),
            pl.BlockSpec(forward.shape, lambda d: (0, 0)),
            pl.BlockSpec(backward.shape, lambda d: (0, 0)),
            pl.BlockSpec(twist.shape, lambda d: (0, 0, 0)),
        ],
        out_specs=pl.BlockSpec((blocks, 1, bins, 2 * lines), lambda d: (0, d, 0, 0)),
        out_shape=jax.ShapeDtypeStruct((blocks, dates, bins, 2 * lines), jnp.float32),
        name="focus",
    )(signal, filt, jnp.asarray(forward), jnp.asarray(backward), jnp.asarray(twist))


def turn_kernel(bins, x_ref, o_ref):
    rows, width = x_ref.shape
    dates, lines = rows // bins, width // 2
    for b in range(bins):
        flat = x_ref[pl.ds(b, dates, stride=bins), :].T
        o_ref[0, b] = flat[:lines]
        o_ref[1, b] = flat[lines:]


def turn(blocks, bins):
    rows, width = blocks.shape
    return pl.pallas_call(
        functools.partial(turn_kernel, bins),
        out_shape=jax.ShapeDtypeStruct((2, bins, width // 2, rows // bins), jnp.float32),
        name="turn",
    )(blocks)


def link_kernel(off_ref, z_ref, s_ref, o_ref, win, mat, tam, mask):
    i, j = pl.program_id(0), pl.program_id(1)
    dates = z_ref.shape[3]

    @pl.when((i == 0) & (j == 0))
    def _():
        pixel = lax.broadcasted_iota(jnp.int32, (PIXELS, SLOTS), 0)
        slot = lax.broadcasted_iota(jnp.int32, (PIXELS, SLOTS), 1)
        line, col = pixel // TILE, pixel % TILE
        slot_col = (slot * 171) >> 11
        slot_line = slot - slot_col * SPAN_ROWS
        inside = (slot < USED) & (slot_line >= line) & (slot_line < line + WIN)
        inside = inside & (slot_col >= col) & (slot_col < col + WIN)
        one = jnp.where(inside, 1.0, 0.0)
        mask[...] = jnp.concatenate([one, one], axis=1)

    first_row = i * HALF + 1 + off_ref[i // 2, j, 0]
    first_col = j * TILE + 1 + off_ref[i // 2, j, 1]
    for c in range(2):
        for b in range(SPAN_COLS):
            win[c, b * SPAN_ROWS : (b + 1) * SPAN_ROWS, :] = z_ref[
                c, first_col + b, pl.ds(first_row, SPAN_ROWS), :
            ]
        win[c, USED:SLOTS, :] = jnp.zeros((SLOTS - USED, dates), jnp.float32)
    zr, zi = win[0], win[1]
    high, low = parts_of(zr * zr + zi * zi)
    picks = mask[...].astype(jnp.bfloat16)
    power = jnp.dot(picks, jnp.concatenate([high, low], axis=0), preferred_element_type=jnp.float32)
    scale = 1.0 / jnp.sqrt(power + 1e-06)
    scale = jnp.concatenate([scale, scale], axis=1)

    whole = jnp.concatenate(
        [jnp.concatenate([zr, zi], axis=1), jnp.concatenate([-zi, zr], axis=1)], axis=0
    )
    high, low = parts_of(whole)
    mat[...] = jnp.concatenate([high, high, low], axis=0)
    tr, ti = zr.T, zi.T
    high, low = parts_of(
        jnp.concatenate(
            [jnp.concatenate([tr, -ti], axis=1), jnp.concatenate([ti, tr], axis=1)], axis=0
        )
    )
    tam[...] = jnp.concatenate([high, high, low], axis=0)

    vec = jnp.concatenate(
        [s_ref[0].reshape(PIXELS, dates), s_ref[1].reshape(PIXELS, dates)], axis=1
    )

    def product(value, table_ref):
        high, low = parts_of(value)
        return jnp.dot(
            jnp.concatenate([high, low, high], axis=1),
            table_ref[...],
            preferred_element_type=jnp.float32,
        )

    for step in range(ITERS):
        proj = product(vec * scale, tam) * mask[...]
        gam = product(proj, mat) * scale
        length = jnp.sqrt(jnp.sum(gam * gam, axis=1, keepdims=True) + 1e-06)
        vec = gam / length
    o_ref[0] = vec[:, :dates].reshape(HALF, TILE, dates)
    o_ref[1] = vec[:, dates:].reshape(HALF, TILE, dates)


def link(window, starts, shifts):
    _, lines, bins, dates = starts.shape
    spec = pl.BlockSpec((2, HALF, TILE, dates), lambda i, j, off: (0, i, j, 0))
    return pl.pallas_call(
        link_kernel,
        grid_spec=pltpu.PrefetchScalarGridSpec(
            num_scalar_prefetch=1,
            grid=(lines // HALF, bins // TILE),
            in_specs=[pl.BlockSpec(window.shape, lambda i, j, off: (0, 0, 0, 0)), spec],
            out_specs=spec,
            scratch_shapes=[
                pltpu.VMEM((2, SLOTS, dates), jnp.float32),
                pltpu.VMEM((6 * SLOTS, 2 * dates), jnp.bfloat16),
                pltpu.VMEM((6 * dates, 2 * SLOTS), jnp.bfloat16),
                pltpu.VMEM((PIXELS, 2 * SLOTS), jnp.float32),
            ],
        ),
        out_shape=jax.ShapeDtypeStruct(starts.shape, jnp.float32),
        name="link",
    )(shifts, window, starts)


def shards(raw_stack, azimuth_filter, start_vectors, window_offsets):
    az_parts = lax.axis_size("az")
    date_parts = lax.axis_size("date")
    bins = raw_stack.shape[2] // az_parts
    lines = raw_stack.shape[3] * az_parts // date_parts
    turned = lax.all_to_all(raw_stack, "az", split_axis=2, concat_axis=3, tiled=True)
    filt_part = lax.dynamic_slice_in_dim(azimuth_filter, lax.axis_index("az") * bins, bins, 1)
    blocks = focus(turned, filt_part, lines)
    blocks = lax.all_to_all(blocks, "date", split_axis=0, concat_axis=0, tiled=True)
    flat = turn(blocks.reshape(-1, 2 * lines), bins)
    window = padded(flat, (("date", 2), ("az", 1)), RIM)
    return link(window, start_vectors, window_offsets)


def solution(mesh):
    placed = (P(None, "date", None, "az"), P(), P(None, "date", "az", None), P("date", "az", None))
    return jax.shard_map(
        shards, mesh=mesh, in_specs=placed, out_specs=P(None, "date", "az", None), check_vma=False
    )
```

time: 533 us -> 135 us (0.25); the launches traced: 523 us -> 134 us
  other arithmetic: 250 us -> 2.4 us
  matrix products: 151 us -> 0 us
  Pallas kernels: 0 us -> 56.5 us
  local copies, waits for them, and re-layouts: 52 us -> 8.65 us
    reduce_sum x40 -> x0, other arithmetic: 238 us -> none  [the longest x32 122 us: link(): jnp.sum(view_real * wgt_real + view_imag * wgt_imag, axis=-1, keepdims=True)]
    dot_general x8 -> x0, matrix products: 151 us -> none  [the longest x4 75.9 us: backward(): return jnp.einsum('dck,ka->acd', field, table, precision=highest)]
    pallas_call x0 -> x3, Pallas kernels: none -> 56.5 us  [the longest x1 46.3 us: link(): pl.pallas_call(link_kernel, grid_spec=pltpu.PrefetchScalarGridSpec(num_sc...]
    unnamed x205 -> x8, local copies, waits for them, and re-layouts: 21.9 us -> 3.54 us
    slice x6 -> x0, local copies, waits for them, and re-layouts: 10.6 us -> none  [the longest x2 3.9 us: link(): imag_z[a:a + side, b:b + side]]
    all_to_all x3 -> x0, local copies, waits for them, and re-layouts: 7.62 us -> none  [shards(): lax.all_to_all(focused, 'date', split_axis=1, concat_axis=3, tiled=True)]
    another operation x1 -> x0, local copies, waits for them, and re-layouts: 6.15 us -> none  [focus(): return jnp.stack([out_real, out_imag])]
  transfers between devices with their start and end apart: 5 -> 5, of which waited for: 4 -> 4; matrix products, arithmetic and copies ran while one was open for 0% -> 2% of each run, Pallas kernels for 0% -> 0%
where the time goes in v1:
time: 135 us; the launch traced here: 134 us
  Pallas kernels  56.5 us (42%)
  blocking collectives  33 us (24%)
  waiting for transfers between devices  21.9 us (16%)
  starting transfers between devices  11.4 us (8%)
  local copies, waits for them, and re-layouts  8.65 us (6%)
  other arithmetic  2.4 us (2%)
    pallas_call x1, Pallas kernels, link(): pl.pallas_call(link_kernel, grid_spec=pltpu.PrefetchScalarGridSpec(num_sc...  46.3 us
    all_to_all x1, blocking collectives, shards(): lax.all_to_all(blocks, 'date', split_axis=0, concat_axis=0, tiled=True)  33 us
    all_to_all x1, waiting for transfers between devices, shards(): lax.all_to_all(raw_stack, 'az', split_axis=2, concat_axis=3, tiled=True)  11.6 us
    pallas_call x1, Pallas kernels, focus(): pl.pallas_call(functools.partial(focus_kernel, lines), grid=(dates,), in_...  7.65 us
    ppermute x2, waiting for transfers between devices, padded(): lax.ppermute(lax.slice_in_dim(block, 0, width, axis=dim), axis, backward)  7.45 us
    ppermute x2, starting transfers between devices, padded(): lax.ppermute(lax.slice_in_dim(block, block.shape[dim] - width, None, axis...  4.57 us
    all_to_all x1, starting transfers between devices, shards(): lax.all_to_all(raw_stack, 'az', split_axis=2, concat_axis=3, tiled=True)  3.58 us
    unnamed x8, local copies, waits for them, and re-layouts  3.54 us
  transfers between devices with their start and end apart: 5, of which 4 were waited for; matrix products, arithmetic and copies ran while one was open for 2% of the time, Pallas kernels for 0%

profile of v1, /device:TPU:9, one launch (start us, length us, event | category | flops | bytes accessed | tf_op | source)
XLA Modules:
  0.0 133.9 jit_solution(5923974694023216776)
XLA Ops:
  0.0 0.0 copy-start
  0.0 2.8 %copy.14 = f32[2,8,32,512]{3,1,0,2:T(8,128)} copy(f32[2,8,32,512]{3,2,1,0:T(8,128)} %param.7) | data formatting | bytes 2097152 | tf_op args[0]
  2.9 3.6 %all-to-all-start = ((f32[2,8,32,512]{3,1,0,2:T(8,128)}), f32[2,8,32,512]{3,1,0,2:T(8,128)S(1)}, u32[]{:S(2)}, u32[]{:S(2)}) async-start(f32[2,8,32,512]{3,1,0,2:T(8,128)} %copy.14), calls=%async_computation | async-start | bytes 2097152 | tf_op jit(solution)/shard_map/all_to_all | solution.py:254
  6.4 0.0 copy-done
  6.5 0.3 copy.16
  6.8 1.0 copy.17
  7.8 11.6 %all-to-all-done = f32[2,8,32,512]{3,1,0,2:T(8,128)S(1)} async-done(((f32[2,8,32,512]{3,1,0,2:T(8,128)}), f32[2,8,32,512]{3,1,0,2:T(8,128)S(1)}, u32[]{:S(2)}, u32[]{:S(2)}) %all-to-all-start) | async-done | bytes 1048608 | tf_op jit(solution)/shard_map/all_to_all | solution.py:254
  19.4 0.8 copy.20
  20.2 1.9 %all_to_all.19.x_ref = f32[2,8,16,1024]{3,2,1,0:T(8,128)} reshape(f32[2,8,16,2,512]{4,3,2,1,0:T(2,128)S(1)} %bitcast.9) | data formatting | bytes 2097152 | tf_op jit(solution)/shard_map/all_to_all | solution.py:254
  22.1 7.6 %focus.1 = f32[16,8,16,128]{3,2,1,0:T(8,128)} custom-call(f32[2,8,16,1024]{3,2,1,0:T(8,128)} %all_to_all.19.x_ref, f32[2,8,16,128]{3,2,1,0:T(8,128)} %bitcast.11, bf16[768,256]{1,0:T(8,128)(2,1)} %constant.16.clone.fwd_ref, bf16[768,256]{1,0:T(8,128)(2,1)} %constant.17.clone.bwd_ref, f32[2,8,128]{2,1,0:T(8,128)} %constant.18.clone.tw_ref), custom_call_target="tpu_custom_call" | custom-call | tf_op jit(solution)/shard_map/focus/pallas_call | solution.py:128
  29.8 33.0 %all_to_all.23 = f32[16,8,16,128]{3,2,1,0:T(8,128)} all-to-all(f32[16,8,16,128]{3,2,1,0:T(8,128)} %focus.1), channel_id=1, replica_groups=mesh['date'=16,'az'=2] {'date'}, dimensions={0} | all-to-all | bytes 2097152 | tf_op jit(solution)/shard_map/all_to_all | solution.py:257
  62.7 0.0 copy-start.2
  62.7 2.6 %turn.1 = f32[2,16,64,128]{3,2,1,0:T(8,128)} custom-call(f32[2048,128]{1,0:T(8,128)} %bitcast.10), custom_call_target="tpu_custom_call" | custom-call | tf_op jit(solution)/shard_map/turn/pallas_call | solution.py:155
  65.3 0.0 copy-start.1
  65.3 1.1 fusion
  66.4 2.6 %collective-permute-start = (f32[2,16,3,128]{3,2,1,0:T(4,128)S(1)}, f32[2,16,3,128]{3,2,1,0:T(4,128)S(1)}, u32[]{:S(2)}, u32[]{:S(2)}) collective-permute-start(f32[2,16,3,128]{3,2,1,0:T(4,128)S(1)} %get-tuple-element.7), channel_id=1, source_target_pairs={{0,2},{2,4},{4,6},{6,8},{8,10},{10,12},{12,14},{14,16},{16,18},{18... | collective-permute-start | bytes 147464 | tf_op jit(solution)/shard_map/ppermute | solution.py:35
  69.0 1.9 %collective-permute-start.1 = (f32[2,16,3,128]{3,2,1,0:T(4,128)S(1)}, f32[2,16,3,128]{3,2,1,0:T(4,128)S(1)}, u32[]{:S(2)}, u32[]{:S(2)}) collective-permute-start(f32[2,16,3,128]{3,2,1,0:T(4,128)S(1)} %get-tuple-element.8), channel_id=1, source_target_pairs={{2,0},{4,2},{6,4},{8,6},{10,8},{12,10},{14,12},{16,14},{18,16},{20... | collective-permute-start | bytes 147464 | tf_op jit(solution)/shard_map/ppermute | solution.py:38
  71.0 0.0 collective-permute-done
  71.0 3.6 %collective-permute-done.1 = f32[2,16,3,128]{3,2,1,0:T(4,128)S(1)} collective-permute-done((f32[2,16,3,128]{3,2,1,0:T(4,128)S(1)}, f32[2,16,3,128]{3,2,1,0:T(4,128)S(1)}, u32[]{:S(2)}, u32[]{:S(2)}) %collective-permute-start.1) | collective-permute-done | bytes 49184 | tf_op jit(solution)/shard_map/ppermute | solution.py:38
  74.6 1.1 pad_maximum_fusion.3
  75.7 1.9 %collective-permute-start.2 = (f32[2,3,70,128]{3,2,1,0:T(8,128)S(1)}, f32[2,3,70,128]{3,2,1,0:T(8,128)S(1)}, u32[]{:S(2)}, u32[]{:S(2)}) collective-permute-start(f32[2,3,70,128]{3,2,1,0:T(8,128)S(1)} %get-tuple-element.5), channel_id=1, source_target_pairs={{0,1},{2,3},{4,5},{6,7},{8,9},{10,11},{12,13},{14,15},{16,17},{18,... | collective-permute-start | bytes 645128 | tf_op jit(solution)/shard_map/ppermute | solution.py:35
  77.6 1.3 collective-permute-start.3
  78.9 0.0 copy-done.2
  78.9 0.7 copy.18.off_ref
  79.6 2.9 %collective-permute-done.2 = f32[2,3,70,128]{3,2,1,0:T(8,128)S(1)} collective-permute-done((f32[2,3,70,128]{3,2,1,0:T(8,128)S(1)}, f32[2,3,70,128]{3,2,1,0:T(8,128)S(1)}, u32[]{:S(2)}, u32[]{:S(2)}) %collective-permute-start.2) | collective-permute-done | bytes 215072 | tf_op jit(solution)/shard_map/ppermute | solution.py:35
  82.5 3.8 %collective-permute-done.3 = f32[2,3,70,128]{3,2,1,0:T(8,128)S(1)} collective-permute-done((f32[2,3,70,128]{3,2,1,0:T(8,128)S(1)}, f32[2,3,70,128]{3,2,1,0:T(8,128)S(1)}, u32[]{:S(2)}, u32[]{:S(2)}) %collective-permute-start.3) | collective-permute-done | bytes 215072 | tf_op jit(solution)/shard_map/ppermute | solution.py:38
  86.3 0.0 copy-done.1
  86.3 1.3 pad_maximum_fusion.z_ref
  87.6 46.3 %link.1 = f32[2,64,16,128]{3,2,1,0:T(8,128)} custom-call(s32[4,1,2]{2,1,0:T(1,128)} %copy.18.off_ref, f32[2,22,70,128]{3,2,1,0:T(8,128)} %pad_maximum_fusion.z_ref, f32[2,64,16,128]{3,2,1,0:T(8,128)} %s_ref.1), custom_call_target="tpu_custom_call" | custom-call | tf_op jit(solution)/shard_map/link/pallas_call | solution.py:230
  (1 shorter events, 0.0 us)
Async XLA Ops:
  0.0 6.4 %copy-start = (f32[2,32,1024]{2,1,0:T(8,128)S(1)}, f32[2,32,1024]{2,1,0:T(8,128)}, u32[]{:S(2)}) copy-start(f32[2,32,1024]{2,1,0:T(8,128)} %param.8) | copy-start | bytes 786436
  2.9 16.6 %all-to-all-start = ((f32[2,8,32,512]{3,1,0,2:T(8,128)}), f32[2,8,32,512]{3,1,0,2:T(8,128)S(1)}, u32[]{:S(2)}, u32[]{:S(2)}) async-start(f32[2,8,32,512]{3,1,0,2:T(8,128)} %copy.14), calls=%async_computation | async-start | bytes 2097152 | tf_op jit(solution)/shard_map/all_to_all | solution.py:254
  62.7 16.2 %copy-start.2 = (s32[4,1,2]{0,2,1:T(2,128)S(1)}, s32[4,1,2]{0,2,1:T(2,128)}, u32[]{:S(2)}) copy-start(s32[4,1,2]{0,2,1:T(2,128)} %param.10) | copy-start | bytes 100
  65.3 21.0 %copy-start.1 = (f32[2,16,64,128]{3,2,1,0:T(8,128)S(1)}, f32[2,16,64,128]{3,2,1,0:T(8,128)}, u32[]{:S(2)}) copy-start(f32[2,16,64,128]{3,2,1,0:T(8,128)} %turn.1) | copy-start | bytes 3145732
  66.4 4.6 %collective-permute-start = (f32[2,16,3,128]{3,2,1,0:T(4,128)S(1)}, f32[2,16,3,128]{3,2,1,0:T(4,128)S(1)}, u32[]{:S(2)}, u32[]{:S(2)}) collective-permute-start(f32[2,16,3,128]{3,2,1,0:T(4,128)S(1)} %get-tuple-element.7), channel_id=1, source_target_pairs={{0,2},{2,4},{4,6},{6,8},{8,10},{10,12},{12,14},{14,16},{16,18},{18... | collective-permute-start | bytes 147464 | tf_op jit(solution)/shard_map/ppermute | solution.py:35
  69.0 5.6 %collective-permute-start.1 = (f32[2,16,3,128]{3,2,1,0:T(4,128)S(1)}, f32[2,16,3,128]{3,2,1,0:T(4,128)S(1)}, u32[]{:S(2)}, u32[]{:S(2)}) collective-permute-start(f32[2,16,3,128]{3,2,1,0:T(4,128)S(1)} %get-tuple-element.8), channel_id=1, source_target_pairs={{2,0},{4,2},{6,4},{8,6},{10,8},{12,10},{14,12},{16,14},{18,16},{20... | collective-permute-start | bytes 147464 | tf_op jit(solution)/shard_map/ppermute | solution.py:38
  75.7 6.8 %collective-permute-start.2 = (f32[2,3,70,128]{3,2,1,0:T(8,128)S(1)}, f32[2,3,70,128]{3,2,1,0:T(8,128)S(1)}, u32[]{:S(2)}, u32[]{:S(2)}) collective-permute-start(f32[2,3,70,128]{3,2,1,0:T(8,128)S(1)} %get-tuple-element.5), channel_id=1, source_target_pairs={{0,1},{2,3},{4,5},{6,7},{8,9},{10,11},{12,13},{14,15},{16,17},{18,... | collective-permute-start | bytes 645128 | tf_op jit(solution)/shard_map/ppermute | solution.py:35
  77.6 8.7 %collective-permute-start.3 = (f32[2,3,70,128]{3,2,1,0:T(8,128)S(1)}, f32[2,3,70,128]{3,2,1,0:T(8,128)S(1)}, u32[]{:S(2)}, u32[]{:S(2)}) collective-permute-start(f32[2,3,70,128]{3,2,1,0:T(8,128)S(1)} %get-tuple-element.6), channel_id=1, source_target_pairs={{1,0},{3,2},{5,4},{7,6},{9,8},{11,10},{13,12},{15,14},{17,16},{19,... | collective-permute-start | bytes 645128 | tf_op jit(solution)/shard_map/ppermute | solution.py:38

commit v2 on v1

v2 whole, which is shorter than its diff:
```python
import functools
import math

import jax
import jax.numpy as jnp
import numpy as np
from jax import lax
from jax.experimental import pallas as pl
from jax.experimental.pallas import tpu as pltpu
from jax.sharding import PartitionSpec as P

TILE = 16
WIN = 5
ITERS = 8
RIM = WIN // 2 + 1
HALF = TILE // 2
SPAN_ROWS = HALF + WIN - 1
SPAN_COLS = TILE + WIN - 1
PIXELS = HALF * TILE
USED = SPAN_ROWS * SPAN_COLS
SLOTS = 256
LANES = 128
GROUP = 4
STACKED = False


def parts_of(value):
    high = value.astype(jnp.bfloat16)
    return high, (value - high.astype(jnp.float32)).astype(jnp.bfloat16)


def butterflies(values, sign):
    count = len(values)
    if count == 1:
        return values
    even = butterflies(values[0::2], sign)
    odd = butterflies(values[1::2], sign)
    low, high = [], []
    for k in range(count // 2):
        (er, ei), (dr, di) = even[k], odd[k]
        if k == 0:
            tr, ti = dr, di
        elif 4 * k == count:
            tr, ti = (-di, dr) if sign > 0 else (di, -dr)
        else:
            c = math.cos(2 * math.pi * k / count)
            s = sign * math.sin(2 * math.pi * k / count)
            tr, ti = dr * c - di * s, dr * s + di * c
        low.append((er + tr, ei + ti))
        high.append((er - tr, ei - ti))
    return low + high


def focus_tables(length):
    radix = length // LANES
    a = np.arange(LANES)
    angle = 2 * np.pi * (np.outer(a, a) % LANES) / LANES
    c, s = np.cos(angle), np.sin(angle)
    forward = np.block([[c, -s], [s, c]])
    backward = np.block([[c, s], [-s, c]])

    def stacked(table):
        high = table.astype(jnp.bfloat16)
        low = (table - high.astype(np.float64)).astype(jnp.bfloat16)
        return np.concatenate([high, high, low], axis=0)

    turn = 2 * np.pi * np.outer(np.arange(radix), a) / length
    twist = np.stack([np.cos(turn), np.sin(turn)]).astype(np.float32)
    return stacked(forward), stacked(backward), twist


def neighbours():
    return [(dd, da) for dd in (-1, 0, 1) for da in (-1, 0, 1) if (dd, da) != (0, 0)]


def exchange_kernel(
    date_parts, az_parts, chunk,
    raw_ref, f_ref, fwd_ref, bwd_ref, tw_ref, z_ref,
    inbox, outbox, mailbox,
    own_sem, az_send, az_recv, date_send, date_recv, rim_send, rim_recv,
):
    _, dates, all_bins, width = raw_ref.shape
    bins = all_bins // az_parts
    length = width * az_parts
    lines = length // date_parts
    radix = length // LANES
    chunks = dates // chunk
    rows = chunk * bins
    block = dates * bins
    my_date, my_az = lax.axis_index("date"), lax.axis_index("az")

    def inside(dd, da):
        date, az = my_date + dd, my_az + da
        return (date >= 0) & (date < date_parts) & (az >= 0) & (az < az_parts)

    def device(date, az):
        return {"date": date, "az": az}

    z_ref[...] = jnp.zeros_like(z_ref)
    barrier = pltpu.get_barrier_semaphore()
    mesh_ids = pl.DeviceIdType.MESH
    expected = date_parts - 1 + az_parts - 1
    for k in range(1, date_parts):
        peer = lax.rem(my_date + k, date_parts)
        pl.semaphore_signal(barrier, inc=1, device_id=device(peer, my_az), device_id_type=mesh_ids)
    for k in range(1, az_parts):
        peer = lax.rem(my_az + k, az_parts)
        pl.semaphore_signal(barrier, inc=1, device_id=device(my_date, peer), device_id_type=mesh_ids)
    for dd, da in neighbours():
        if dd != 0 and da != 0:
            there = inside(dd, da)
            expected = expected + there.astype(jnp.int32)

            @pl.when(there)
            def _():
                pl.semaphore_signal(
                    barrier,
                    inc=1,
                    device_id=device(my_date + dd, my_az + da),
                    device_id_type=mesh_ids,
                )

    pl.semaphore_wait(barrier, expected)

    def az_copy(step, peer):
        return pltpu.make_async_remote_copy(
            src_ref=raw_ref.at[
                :, pl.ds(step * chunk, chunk), pl.ds(pl.multiple_of(peer * bins, 8), bins), :
            ],
            dst_ref=inbox.at[my_az, :, pl.ds(step * chunk, chunk)],
            send_sem=az_send.at[step, peer],
            recv_sem=az_recv.at[step, my_az],
            device_id=device(my_date, peer),
            device_id_type=mesh_ids,
        )

    def az_arrival(step, peer):
        return pltpu.make_async_remote_copy(
            src_ref=raw_ref.at[:, pl.ds(step * chunk, chunk), pl.ds(0, bins), :],
            dst_ref=inbox.at[peer, :, pl.ds(step * chunk, chunk)],
            send_sem=az_send.at[step, peer],
            recv_sem=az_recv.at[step, peer],
            device_id=device(my_date, peer),
            device_id_type=mesh_ids,
        )

    for step in range(chunks):
        for k in range(1, az_parts):
            az_copy(step, lax.rem(my_az + k, az_parts)).start()
    own = pltpu.make_async_copy(
        raw_ref.at[:, :, pl.ds(pl.multiple_of(my_az * bins, 8), bins), :],
        inbox.at[my_az],
        own_sem.at[0],
    )
    own.start()
    own.wait()

    def product(value, table_ref):
        high, low = parts_of(value)
        return jnp.dot(
            jnp.concatenate([high, low, high], axis=1),
            table_ref[...],
            preferred_element_type=jnp.float32,
        )

    def date_copy(peer, start, size):
        return pltpu.make_async_remote_copy(
            src_ref=outbox.at[peer, pl.ds(start, size), :],
            dst_ref=mailbox.at[pl.ds(pl.multiple_of(my_date * block + start, 8), size), :],
            send_sem=date_send.at[peer],
            recv_sem=date_recv.at[my_date],
            device_id=device(peer, my_az),
            device_id_type=mesh_ids,
        )

    def date_arrival(peer):
        return pltpu.make_async_remote_copy(
            src_ref=outbox.at[peer],
            dst_ref=mailbox.at[pl.ds(pl.multiple_of(peer * block, 8), block), :],
            send_sem=date_send.at[peer],
            recv_sem=date_recv.at[peer],
            device_id=device(peer, my_az),
            device_id_type=mesh_ids,
        )

    @pl.loop(0, chunks)
    def _(step):
        for k in range(1, az_parts):
            az_arrival(step, lax.rem(my_az + k, az_parts)).wait_recv()
        field = []
        for b in range(radix):
            source, at = b * LANES // width, b * LANES % width
            field.append(
                tuple(
                    inbox[source, c, pl.ds(step * chunk, chunk), :, at : at + LANES].reshape(
                        rows, LANES
                    )
                    for c in range(2)
                )
            )
        stack = []
        for k, (re, im) in enumerate(butterflies(field, -1)):
            c, s = tw_ref[0, k : k + 1, :], tw_ref[1, k : k + 1, :]
            stack.append(jnp.concatenate([re * c + im * s, im * c - re * s], axis=1))
        spec = product(jnp.concatenate(stack, axis=0), fwd_ref)
        sr, si = spec[:, :LANES], spec[:, LANES:]
        full = (radix, chunk, bins, LANES)
        fr = jnp.broadcast_to(f_ref[0][:, None], full).reshape(radix * rows, LANES)
        fi = jnp.broadcast_to(f_ref[1][:, None], full).reshape(radix * rows, LANES)
        back = product(jnp.concatenate([sr * fr - si * fi, sr * fi + si * fr], axis=1), bwd_ref)
        inverse = 1.0 / length
        field = []
        for k in range(radix):
            c, s = tw_ref[0, k : k + 1, :] * inverse, tw_ref[1, k : k + 1, :] * inverse
            re = back[k * rows : (k + 1) * rows, :LANES]
            im = back[k * rows : (k + 1) * rows, LANES:]
            field.append((re * c - im * s, im * c + re * s))
        field = butterflies(field, 1)
        start = pl.multiple_of(step * rows, 8)
        for place in range(date_parts):
            b, low = place * lines // LANES, place * lines % LANES
            re, im = field[b]
            outbox[place, pl.ds(start, rows), :] = jnp.concatenate(
                [re[:, low : low + lines], im[:, low : low + lines]], axis=1
            )
        for k in range(1, date_parts):
            date_copy(lax.rem(my_date + k, date_parts), start, rows).start()

    keep = pltpu.make_async_copy(
        outbox.at[my_date],
        mailbox.at[pl.ds(pl.multiple_of(my_date * block, 8), block), :],
        own_sem.at[1],
    )
    keep.start()
    keep.wait()
    for k in range(1, date_parts):
        date_arrival(lax.rem(my_date + k, date_parts)).wait_recv()

    def rim_copy(n, dd, da):
        lines_at = {-1: (8, 8 + lines, 8), 0: (8, 8, lines), 1: (lines, 0, 8)}[dd]
        bins_at = {-1: (RIM, RIM + bins, RIM), 0: (RIM, RIM, bins), 1: (bins, 0, RIM)}[da]
        return pltpu.make_async_remote_copy(
            src_ref=z_ref.at[:, pl.ds(bins_at[0], bins_at[2]), pl.ds(lines_at[0], lines_at[2]), :],
            dst_ref=z_ref.at[:, pl.ds(bins_at[1], bins_at[2]), pl.ds(lines_at[1], lines_at[2]), :],
            send_sem=rim_send.at[n],
            recv_sem=rim_recv.at[n],
            device_id=device(my_date + dd, my_az + da),
            device_id_type=mesh_ids,
        )

    def send_rims(side):
        for n, (dd, da) in enumerate(neighbours()):
            if da == side:

                @pl.when(inside(dd, da))
                def _():
                    rim_copy(n, dd, da).start()

    edge = list(range(RIM)) + list(range(bins - RIM, bins)) + list(range(RIM, bins - RIM))
    for count, b in enumerate(edge):
        flat = mailbox[pl.ds(b, date_parts * dates, stride=bins), :].T
        z_ref[0, RIM + b, 8 : 8 + lines, :] = flat[:lines]
        z_ref[1, RIM + b, 8 : 8 + lines, :] = flat[lines:]
        if count == RIM - 1:
            send_rims(-1)
        if count == 2 * RIM - 1:
            send_rims(1)
    send_rims(0)

    for step in range(chunks):
        for k in range(1, az_parts):
            az_copy(step, lax.rem(my_az + k, az_parts)).wait_send()
    for k in range(1, date_parts):
        date_arrival(lax.rem(my_date + k, date_parts)).wait_send()
    for n, (dd, da) in enumerate(neighbours()):

        @pl.when(inside(dd, da))
        def _():
            rim_copy(n, dd, da).wait_send()

        @pl.when(inside(-dd, -da))
        def _():
            rim_copy(n, dd, da).wait_recv()


def exchange(raw, filt):
    az_parts, date_parts = lax.axis_size("az"), lax.axis_size("date")
    _, dates, all_bins, width = raw.shape
    bins, length = all_bins // az_parts, width * az_parts
    lines, radix = length // date_parts, length // LANES
    chunk = 2 if dates % 2 == 0 else 1
    forward, backward, twist = focus_tables(length)
    filt = filt.reshape(2, bins, LANES, radix).transpose(0, 3, 1, 2)
    near = pl.BlockSpec(memory_space=pltpu.VMEM)
    dma = pltpu.SemaphoreType.DMA
    return pl.pallas_call(
        functools.partial(exchange_kernel, date_parts, az_parts, chunk),
        in_specs=[pl.BlockSpec(memory_space=pl.ANY)] + [near] * 4,
        out_specs=near,
        out_shape=jax.ShapeDtypeStruct(
            (2, bins + 2 * RIM, lines + 16, date_parts * dates), jnp.float32
        ),
        scratch_shapes=[
            pltpu.VMEM((az_parts, 2, dates, bins, width), jnp.float32),
            pltpu.VMEM((date_parts, dates * bins, 2 * lines), jnp.float32),
            pltpu.VMEM((date_parts * dates * bins, 2 * lines), jnp.float32),
            dma((2,)),
            dma((dates // chunk, az_parts)),
            dma((dates // chunk, az_parts)),
            dma((date_parts,)),
            dma((date_parts,)),
            dma((8,)),
            dma((8,)),
        ],
        compiler_params=pltpu.CompilerParams(
            collective_id=0, has_side_effects=True, vmem_limit_bytes=40 * 1024 * 1024
        ),
        name="exchange",
    )(raw, filt, jnp.asarray(forward), jnp.asarray(backward), jnp.asarray(twist))


def link_kernel(off_ref, z_ref, s_ref, o_ref, win, mat, tam, mask):
    i, j = pl.program_id(0), pl.program_id(1)
    dates = z_ref.shape[3]

    @pl.when((i == 0) & (j == 0))
    def _():
        pixel = lax.broadcasted_iota(jnp.int32, (PIXELS, SLOTS), 0)
        slot = lax.broadcasted_iota(jnp.int32, (PIXELS, SLOTS), 1)
        line, col = pixel // TILE, pixel % TILE
        slot_col = (slot * 171) >> 11
        slot_line = slot - slot_col * SPAN_ROWS
        inside = (slot < USED) & (slot_line >= line) & (slot_line < line + WIN)
        inside = inside & (slot_col >= col) & (slot_col < col + WIN)
        one = jnp.where(inside, 1.0, 0.0)
        mask[...] = jnp.concatenate([one, one], axis=1)

    def product(value, table_ref):
        high, low = parts_of(value)
        if STACKED:
            rows, depth = value.shape
            both = jnp.dot(
                jnp.concatenate([high, low], axis=0),
                table_ref[:depth],
                preferred_element_type=jnp.float32,
            )
            rest = jnp.dot(high, table_ref[depth:], preferred_element_type=jnp.float32)
            return both[:rows] + (both[rows:] + rest)
        return jnp.dot(
            jnp.concatenate([high, low, high], axis=1),
            table_ref[...],
            preferred_element_type=jnp.float32,
        )

    def stacked(high, low):
        return jnp.concatenate([high, low] if STACKED else [high, high, low], axis=0)

    vecs, scales = [], []
    for g in range(GROUP):
        number = i * GROUP + g
        first_row = number * HALF + 9 - RIM + off_ref[number // 2, j, 0]
        first_col = j * TILE + 1 + off_ref[number // 2, j, 1]
        for c in range(2):
            for b in range(SPAN_COLS):
                win[g, c, b * SPAN_ROWS : (b + 1) * SPAN_ROWS, :] = z_ref[
                    c, first_col + b, pl.ds(first_row, SPAN_ROWS), :
                ]
            win[g, c, USED:SLOTS, :] = jnp.zeros((SLOTS - USED, dates), jnp.float32)
        zr, zi = win[g, 0], win[g, 1]
        picks = mask[...].astype(jnp.bfloat16)
        power = jnp.dot(
            picks,
            jnp.concatenate(parts_of(zr * zr + zi * zi), axis=0),
            preferred_element_type=jnp.float32,
        )
        scale = 1.0 / jnp.sqrt(power + 1e-06)
        scales.append(jnp.concatenate([scale, scale], axis=1))

        whole = jnp.concatenate(
            [jnp.concatenate([zr, zi], axis=1), jnp.concatenate([-zi, zr], axis=1)], axis=0
        )
        mat[g] = stacked(*parts_of(whole))
        tr, ti = zr.T, zi.T
        whole = jnp.concatenate(
            [jnp.concatenate([tr, -ti], axis=1), jnp.concatenate([ti, tr], axis=1)], axis=0
        )
        tam[g] = stacked(*parts_of(whole))
        rows = slice(g * HALF, (g + 1) * HALF)
        vecs.append(
            jnp.concatenate(
                [s_ref[0, rows].reshape(PIXELS, dates), s_ref[1, rows].reshape(PIXELS, dates)],
                axis=1,
            )
        )

    for step in range(ITERS):
        projs = [product(vecs[g] * scales[g], tam.at[g]) * mask[...] for g in range(GROUP)]
        for g in range(GROUP):
            gam = product(projs[g], mat.at[g]) * scales[g]
            total = jnp.sum(gam * gam, axis=1, keepdims=True) + 1e-06
            vecs[g] = gam * (1.0 / jnp.sqrt(total))
    for g in range(GROUP):
        rows = slice(g * HALF, (g + 1) * HALF)
        o_ref[0, rows] = vecs[g][:, :dates].reshape(HALF, TILE, dates)
        o_ref[1, rows] = vecs[g][:, dates:].reshape(HALF, TILE, dates)


def link(window, starts, shifts):
    _, lines, bins, dates = starts.shape
    copies = 2 if STACKED else 3
    spec = pl.BlockSpec((2, GROUP * HALF, TILE, dates), lambda i, j, off: (0, i, j, 0))
    return pl.pallas_call(
        link_kernel,
        grid_spec=pltpu.PrefetchScalarGridSpec(
            num_scalar_prefetch=1,
            grid=(lines // (GROUP * HALF), bins // TILE),
            in_specs=[pl.BlockSpec(window.shape, lambda i, j, off: (0, 0, 0, 0)), spec],
            out_specs=spec,
            scratch_shapes=[
                pltpu.VMEM((GROUP, 2, SLOTS, dates), jnp.float32),
                pltpu.VMEM((GROUP, copies * 2 * SLOTS, 2 * dates), jnp.bfloat16),
                pltpu.VMEM((GROUP, copies * 2 * dates, 2 * SLOTS), jnp.bfloat16),
                pltpu.VMEM((PIXELS, 2 * SLOTS), jnp.float32),
            ],
        ),
        out_shape=jax.ShapeDtypeStruct(starts.shape, jnp.float32),
        compiler_params=pltpu.CompilerParams(vmem_limit_bytes=40 * 1024 * 1024),
        name="link",
    )(shifts, window, starts)


def shards(raw_stack, azimuth_filter, start_vectors, window_offsets):
    bins = raw_stack.shape[2] // lax.axis_size("az")
    filt_part = lax.dynamic_slice_in_dim(azimuth_filter, lax.axis_index("az") * bins, bins, 1)
    window = exchange(raw_stack, filt_part)
    return link(window, start_vectors, window_offsets)


def solution(mesh):
    placed = (P(None, "date", None, "az"), P(), P(None, "date", "az", None), P("date", "az", None))
    return jax.shard_map(
        shards, mesh=mesh, in_specs=placed, out_specs=P(None, "date", "az", None), check_vma=False
    )
```

time: 135 us -> 60.9 us (0.45)
  the two profiles are of different devices: /device:TPU:9 before, /device:TPU:0 now
where the time goes in v2:
time: 60.9 us; the launch traced here: 60.8 us
  Pallas kernels  59.1 us (97%)
  local copies, waits for them, and re-layouts  1.63 us (3%)
    pallas_call x1, Pallas kernels, exchange(): pl.pallas_call(functools.partial(exchange_kernel, date_parts, az_parts, c...  41.9 us
    pallas_call x1, Pallas kernels, link(): pl.pallas_call(link_kernel, grid_spec=pltpu.PrefetchScalarGridSpec(num_sc...  17.1 us

profile of v2, /device:TPU:0, one launch (start us, length us, event | category | flops | bytes accessed | tf_op | source)
XLA Modules:
  0.0 60.8 jit_solution(15042366778279823038)
XLA Ops:
  0.0 0.0 copy-start
  0.0 0.0 copy-start.5
  0.0 0.0 copy-start.3
  0.0 0.0 copy-start.4
  0.0 0.0 copy-start.1
  0.0 0.9 %copy.11.off_ref = s32[4,1,2]{2,1,0:T(1,128)S(1)} copy(s32[4,1,2]{0,2,1:T(2,128)} %param.10) | data formatting | bytes 64 | tf_op args[3]
  0.9 0.0 copy-done
  1.0 0.3 copy.9
  1.3 0.3 copy.10
  1.6 0.0 copy-done.5
  1.6 0.0 copy-done.3
  1.6 0.0 copy-done.4
  1.7 0.0 copy-done.1
  1.7 0.0 copy-start.2
  1.7 41.9 %exchange.1.z_ref = f32[2,22,80,128]{3,2,1,0:T(8,128)S(1)} custom-call(f32[2,8,32,512]{3,2,1,0:T(8,128)S(1)} %copy-done.1, f32[2,8,16,128]{3,2,1,0:T(8,128)S(1)} %bitcast.2, bf16[768,256]{1,0:T(8,128)(2,1)S(1)} %copy-done.4, bf16[768,256]{1,0:T(8,128)(2,1)S(1)} %copy-done.3, f32[2,8,128]{2,1,0:T(8,128)S(1)} %copy-done.5), custom_call_target="tpu_custom_call" | custom-call | tf_op jit(solution)/shard_map/exchange/pallas_call | solution.py:296
  43.6 0.0 copy-done.2
  43.6 17.1 %link.1 = f32[2,64,16,128]{3,2,1,0:T(8,128)} custom-call(s32[4,1,2]{2,1,0:T(1,128)S(1)} %copy.11.off_ref, f32[2,22,80,128]{3,2,1,0:T(8,128)S(1)} %exchange.1.z_ref, f32[2,64,16,128]{3,2,1,0:T(8,128)S(1)} %copy-done.2), custom_call_target="tpu_custom_call" | custom-call | tf_op jit(solution)/shard_map/link/pallas_call | solution.py:412
  (1 shorter events, 0.0 us)
Async XLA Ops:
  0.0 1.0 %copy-start = (f32[2,32,1024]{2,1,0:T(8,128)S(1)}, f32[2,32,1024]{2,1,0:T(8,128)}, u32[]{:S(2)}) copy-start(f32[2,32,1024]{2,1,0:T(8,128)} %param.8) | copy-start | bytes 786436
  0.0 1.6 %copy-start.5 = (f32[2,8,128]{2,1,0:T(8,128)S(1)}, f32[2,8,128]{2,1,0:T(8,128)}, u32[]{:S(2)}) copy-start(f32[2,8,128]{2,1,0:T(8,128)} %constant.18.clone.tw_ref) | copy-start | bytes 24580
  0.0 1.6 %copy-start.3 = (bf16[768,256]{1,0:T(8,128)(2,1)S(1)}, bf16[768,256]{1,0:T(8,128)(2,1)}, u32[]{:S(2)}) copy-start(bf16[768,256]{1,0:T(8,128)(2,1)} %constant.17.clone.bwd_ref) | copy-start | bytes 1179652
  0.0 1.6 %copy-start.4 = (bf16[768,256]{1,0:T(8,128)(2,1)S(1)}, bf16[768,256]{1,0:T(8,128)(2,1)}, u32[]{:S(2)}) copy-start(bf16[768,256]{1,0:T(8,128)(2,1)} %constant.16.clone.fwd_ref) | copy-start | bytes 1179652
  0.0 1.6 %copy-start.1 = (f32[2,8,32,512]{3,2,1,0:T(8,128)S(1)}, f32[2,8,32,512]{3,2,1,0:T(8,128)}, u32[]{:S(2)}) copy-start(f32[2,8,32,512]{3,2,1,0:T(8,128)} %raw_ref.1) | copy-start | bytes 3145732
  1.7 41.9 %copy-start.2 = (f32[2,64,16,128]{3,2,1,0:T(8,128)S(1)}, f32[2,64,16,128]{3,2,1,0:T(8,128)}, u32[]{:S(2)}) copy-start(f32[2,64,16,128]{3,2,1,0:T(8,128)} %s_ref.1) | copy-start | bytes 3145732

commit v3 on v2

--- a/solution.py
+++ b/solution.py
@@ -76,8 +76,8 @@
 def exchange_kernel(
     date_parts, az_parts, chunk,
     raw_ref, f_ref, fwd_ref, bwd_ref, tw_ref, z_ref,
-    inbox, outbox, mailbox,
-    own_sem, az_send, az_recv, date_send, date_recv, rim_send, rim_recv,
+    inbox, outbox, mailbox, rim_out, rim_in,
+    own_sem, az_send, az_recv, date_send, date_recv, rim_send, rim_recv, x_send, x_recv,
 ):
     _, dates, all_bins, width = raw_ref.shape
     bins = all_bins // az_parts
@@ -232,9 +232,38 @@
         own_sem.at[1],
     )
     keep.start()
+
+    def side_copy(side, out, into, landing):
+        return pltpu.make_async_remote_copy(
+            src_ref=out,
+            dst_ref=into,
+            send_sem=x_send.at[side],
+            recv_sem=x_recv.at[landing],
+            device_id=device(my_date, my_az + 2 * side - 1),
+            device_id_type=mesh_ids,
+        )
+
+    def forward(source):
+        for side in range(2):
+
+            @pl.when(inside(0, 2 * side - 1))
+            def _():
+                for n in range(RIM):
+                    b = n + side * (bins - RIM)
+                    rim_out[side, source, n * dates : (n + 1) * dates, :] = mailbox[
+                        pl.ds(source * block + b, dates, stride=bins), :
+                    ]
+                side_copy(
+                    side, rim_out.at[side, source], rim_in.at[1 - side, source], 1 - side
+                ).start()
+
     keep.wait()
+    forward(my_date)
     for k in range(1, date_parts):
-        date_arrival(lax.rem(my_date + k, date_parts)).wait_recv()
+        shift = (k + 1) // 2 if k % 2 else date_parts - k // 2
+        peer = lax.rem(my_date + shift, date_parts)
+        date_arrival(peer).wait_recv()
+        forward(peer)
 
     def rim_copy(n, dd, da):
         lines_at = {-1: (8, 8 + lines, 8), 0: (8, 8, lines), 1: (lines, 0, 8)}[dd]
@@ -250,7 +279,7 @@
 
     def send_rims(side):
         for n, (dd, da) in enumerate(neighbours()):
-            if da == side:
+            if da == side and dd != 0:
 
                 @pl.when(inside(dd, da))
                 def _():
@@ -266,6 +295,19 @@
         if count == 2 * RIM - 1:
             send_rims(1)
     send_rims(0)
+    for side in range(2):
+
+        @pl.when(inside(0, 2 * side - 1))
+        def _():
+            arrival = side_copy(side, rim_out.at[side], rim_in.at[side], side)
+            arrival.wait_recv()
+            for n in range(RIM):
+                flat = rim_in[side, :, n * dates : (n + 1) * dates, :]
+                flat = flat.reshape(date_parts * dates, 2 * lines).T
+                place = n + side * (RIM + bins)
+                z_ref[0, place, 8 : 8 + lines, :] = flat[:lines]
+                z_ref[1, place, 8 : 8 + lines, :] = flat[lines:]
+            arrival.wait_send()
 
     for step in range(chunks):
         for k in range(1, az_parts):
@@ -273,6 +315,8 @@
     for k in range(1, date_parts):
         date_arrival(lax.rem(my_date + k, date_parts)).wait_send()
     for n, (dd, da) in enumerate(neighbours()):
+        if dd == 0:
+            continue
 
         @pl.when(inside(dd, da))
         def _():
@@ -304,6 +348,8 @@
             pltpu.VMEM((az_parts, 2, dates, bins, width), jnp.float32),
             pltpu.VMEM((date_parts, dates * bins, 2 * lines), jnp.float32),
             pltpu.VMEM((date_parts * dates * bins, 2 * lines), jnp.float32),
+            pltpu.VMEM((2, date_parts, RIM * dates, 2 * lines), jnp.float32),
+            pltpu.VMEM((2, date_parts, RIM * dates, 2 * lines), jnp.float32),
             dma((2,)),
             dma((dates // chunk, az_parts)),
             dma((dates // chunk, az_parts)),
@@ -311,6 +357,8 @@
             dma((date_parts,)),
             dma((8,)),
             dma((8,)),
+            dma((2,)),
+            dma((2,)),
         ],
         compiler_params=pltpu.CompilerParams(
             collective_id=0, has_side_effects=True, vmem_limit_bytes=40 * 1024 * 1024

time: 60.9 us -> 59.8 us (0.982)
  the two profiles are of different devices: /device:TPU:0 before, /device:TPU:9 now
where the time goes in v3:
time: 59.8 us; the launch traced here: 59.6 us
  Pallas kernels  57.9 us (97%)
  local copies, waits for them, and re-layouts  1.62 us (3%)
    pallas_call x1, Pallas kernels, exchange(): pl.pallas_call(functools.partial(exchange_kernel, date_parts, az_parts, c...  40.8 us
    pallas_call x1, Pallas kernels, link(): pl.pallas_call(link_kernel, grid_spec=pltpu.PrefetchScalarGridSpec(num_sc...  17.1 us

profile of v3, /device:TPU:9, one launch (start us, length us, event | category | flops | bytes accessed | tf_op | source)
XLA Modules:
  0.0 59.6 jit_solution(7716301032377360213)
XLA Ops:
  0.0 0.0 copy-start
  0.0 0.0 copy-start.5
  0.0 0.0 copy-start.3
  0.0 0.0 copy-start.4
  0.0 0.0 copy-start.1
  0.0 0.9 %copy.11.off_ref = s32[4,1,2]{2,1,0:T(1,128)S(1)} copy(s32[4,1,2]{0,2,1:T(2,128)} %param.10) | data formatting | bytes 64 | tf_op args[3]
  0.9 0.0 copy-done
  1.0 0.3 copy.9
  1.3 0.3 copy.10
  1.6 0.0 copy-done.5
  1.6 0.0 copy-done.3
  1.6 0.0 copy-done.4
  1.7 0.0 copy-done.1
  1.7 0.0 copy-start.2
  1.7 40.8 %exchange.1.z_ref = f32[2,22,80,128]{3,2,1,0:T(8,128)S(1)} custom-call(f32[2,8,32,512]{3,2,1,0:T(8,128)S(1)} %copy-done.1, f32[2,8,16,128]{3,2,1,0:T(8,128)S(1)} %bitcast.2, bf16[768,256]{1,0:T(8,128)(2,1)S(1)} %copy-done.4, bf16[768,256]{1,0:T(8,128)(2,1)S(1)} %copy-done.3, f32[2,8,128]{2,1,0:T(8,128)S(1)} %copy-done.5), custom_call_target="tpu_custom_call" | custom-call | tf_op jit(solution)/shard_map/exchange/pallas_call | solution.py:340
  42.5 0.0 copy-done.2
  42.5 17.1 %link.1 = f32[2,64,16,128]{3,2,1,0:T(8,128)} custom-call(s32[4,1,2]{2,1,0:T(1,128)S(1)} %copy.11.off_ref, f32[2,22,80,128]{3,2,1,0:T(8,128)S(1)} %exchange.1.z_ref, f32[2,64,16,128]{3,2,1,0:T(8,128)S(1)} %copy-done.2), custom_call_target="tpu_custom_call" | custom-call | tf_op jit(solution)/shard_map/link/pallas_call | solution.py:460
  (1 shorter events, 0.0 us)
Async XLA Ops:
  0.0 1.0 %copy-start = (f32[2,32,1024]{2,1,0:T(8,128)S(1)}, f32[2,32,1024]{2,1,0:T(8,128)}, u32[]{:S(2)}) copy-start(f32[2,32,1024]{2,1,0:T(8,128)} %param.8) | copy-start | bytes 786436
  0.0 1.6 %copy-start.5 = (f32[2,8,128]{2,1,0:T(8,128)S(1)}, f32[2,8,128]{2,1,0:T(8,128)}, u32[]{:S(2)}) copy-start(f32[2,8,128]{2,1,0:T(8,128)} %constant.18.clone.tw_ref) | copy-start | bytes 24580
  0.0 1.6 %copy-start.3 = (bf16[768,256]{1,0:T(8,128)(2,1)S(1)}, bf16[768,256]{1,0:T(8,128)(2,1)}, u32[]{:S(2)}) copy-start(bf16[768,256]{1,0:T(8,128)(2,1)} %constant.17.clone.bwd_ref) | copy-start | bytes 1179652
  0.0 1.6 %copy-start.4 = (bf16[768,256]{1,0:T(8,128)(2,1)S(1)}, bf16[768,256]{1,0:T(8,128)(2,1)}, u32[]{:S(2)}) copy-start(bf16[768,256]{1,0:T(8,128)(2,1)} %constant.16.clone.fwd_ref) | copy-start | bytes 1179652
  0.0 1.6 %copy-start.1 = (f32[2,8,32,512]{3,2,1,0:T(8,128)S(1)}, f32[2,8,32,512]{3,2,1,0:T(8,128)}, u32[]{:S(2)}) copy-start(f32[2,8,32,512]{3,2,1,0:T(8,128)} %raw_ref.1) | copy-start | bytes 3145732
  1.7 40.8 %copy-start.2 = (f32[2,64,16,128]{3,2,1,0:T(8,128)S(1)}, f32[2,64,16,128]{3,2,1,0:T(8,128)}, u32[]{:S(2)}) copy-start(f32[2,64,16,128]{3,2,1,0:T(8,128)} %s_ref.1) | copy-start | bytes 3145732

commit v4 on v3

--- a/solution.py
+++ b/solution.py
@@ -20,7 +20,7 @@
 USED = SPAN_ROWS * SPAN_COLS
 SLOTS = 256
 LANES = 128
-GROUP = 4
+GROUP = 8
 STACKED = False
 
 
@@ -369,7 +369,7 @@
 
 def link_kernel(off_ref, z_ref, s_ref, o_ref, win, mat, tam, mask):
     i, j = pl.program_id(0), pl.program_id(1)
-    dates = z_ref.shape[3]
+    dates, group = z_ref.shape[3], s_ref.shape[1] // HALF
 
     @pl.when((i == 0) & (j == 0))
     def _():
@@ -404,8 +404,8 @@
         return jnp.concatenate([high, low] if STACKED else [high, high, low], axis=0)
 
     vecs, scales = [], []
-    for g in range(GROUP):
-        number = i * GROUP + g
+    for g in range(group):
+        number = i * group + g
         first_row = number * HALF + 9 - RIM + off_ref[number // 2, j, 0]
         first_col = j * TILE + 1 + off_ref[number // 2, j, 1]
         for c in range(2):
@@ -442,12 +442,12 @@
         )
 
     for step in range(ITERS):
-        projs = [product(vecs[g] * scales[g], tam.at[g]) * mask[...] for g in range(GROUP)]
-        for g in range(GROUP):
+        projs = [product(vecs[g] * scales[g], tam.at[g]) * mask[...] for g in range(group)]
+        for g in range(group):
             gam = product(projs[g], mat.at[g]) * scales[g]
             total = jnp.sum(gam * gam, axis=1, keepdims=True) + 1e-06
             vecs[g] = gam * (1.0 / jnp.sqrt(total))
-    for g in range(GROUP):
+    for g in range(group):
         rows = slice(g * HALF, (g + 1) * HALF)
         o_ref[0, rows] = vecs[g][:, :dates].reshape(HALF, TILE, dates)
         o_ref[1, rows] = vecs[g][:, dates:].reshape(HALF, TILE, dates)
@@ -456,18 +456,19 @@
 def link(window, starts, shifts):
     _, lines, bins, dates = starts.shape
     copies = 2 if STACKED else 3
-    spec = pl.BlockSpec((2, GROUP * HALF, TILE, dates), lambda i, j, off: (0, i, j, 0))
+    group = math.gcd(GROUP, lines // HALF)
+    spec = pl.BlockSpec((2, group * HALF, TILE, dates), lambda i, j, off: (0, i, j, 0))
     return pl.pallas_call(
         link_kernel,
         grid_spec=pltpu.PrefetchScalarGridSpec(
             num_scalar_prefetch=1,
-            grid=(lines // (GROUP * HALF), bins // TILE),
+            grid=(lines // (group * HALF), bins // TILE),
             in_specs=[pl.BlockSpec(window.shape, lambda i, j, off: (0, 0, 0, 0)), spec],
             out_specs=spec,
             scratch_shapes=[
-                pltpu.VMEM((GROUP, 2, SLOTS, dates), jnp.float32),
-                pltpu.VMEM((GROUP, copies * 2 * SLOTS, 2 * dates), jnp.bfloat16),
-                pltpu.VMEM((GROUP, copies * 2 * dates, 2 * SLOTS), jnp.bfloat16),
+                pltpu.VMEM((group, 2, SLOTS, dates), jnp.float32),
+                pltpu.VMEM((group, copies * 2 * SLOTS, 2 * dates), jnp.bfloat16),
+                pltpu.VMEM((group, copies * 2 * dates, 2 * SLOTS), jnp.bfloat16),
                 pltpu.VMEM((PIXELS, 2 * SLOTS), jnp.float32),
             ],
         ),

time: 59.8 us -> 59.3 us (level)
  no operation moved by 1% of the time
where the time goes in v4:
time: 59.3 us; the launch traced here: 59.1 us
  Pallas kernels  57.4 us (97%)
  local copies, waits for them, and re-layouts  1.62 us (3%)
    pallas_call x1, Pallas kernels, exchange(): pl.pallas_call(functools.partial(exchange_kernel, date_parts, az_parts, c...  40.8 us
    pallas_call x1, Pallas kernels, link(): pl.pallas_call(link_kernel, grid_spec=pltpu.PrefetchScalarGridSpec(num_sc...  16.6 us

profile of v4, /device:TPU:9, one launch (start us, length us, event | category | flops | bytes accessed | tf_op | source)
XLA Modules:
  0.0 59.1 jit_solution(14100610928061374784)
XLA Ops:
  0.0 0.0 copy-start
  0.0 0.0 copy-start.5
  0.0 0.0 copy-start.3
  0.0 0.0 copy-start.4
  0.0 0.0 copy-start.1
  0.0 0.9 %copy.11.off_ref = s32[4,1,2]{2,1,0:T(1,128)S(1)} copy(s32[4,1,2]{0,2,1:T(2,128)} %param.10) | data formatting | bytes 64 | tf_op args[3]
  0.9 0.0 copy-done
  1.0 0.3 copy.9
  1.3 0.3 copy.10
  1.6 0.0 copy-done.5
  1.6 0.0 copy-done.3
  1.6 0.0 copy-done.4
  1.7 0.0 copy-done.1
  1.7 0.0 copy-start.2
  1.7 40.8 %exchange.1.z_ref = f32[2,22,80,128]{3,2,1,0:T(8,128)S(1)} custom-call(f32[2,8,32,512]{3,2,1,0:T(8,128)S(1)} %copy-done.1, f32[2,8,16,128]{3,2,1,0:T(8,128)S(1)} %bitcast.2, bf16[768,256]{1,0:T(8,128)(2,1)S(1)} %copy-done.4, bf16[768,256]{1,0:T(8,128)(2,1)S(1)} %copy-done.3, f32[2,8,128]{2,1,0:T(8,128)S(1)} %copy-done.5), custom_call_target="tpu_custom_call" | custom-call | tf_op jit(solution)/shard_map/exchange/pallas_call | solution.py:340
  42.5 0.0 copy-done.2
  42.5 16.6 %link.1 = f32[2,64,16,128]{3,2,1,0:T(8,128)} custom-call(s32[4,1,2]{2,1,0:T(1,128)S(1)} %copy.11.off_ref, f32[2,22,80,128]{3,2,1,0:T(8,128)S(1)} %exchange.1.z_ref, f32[2,64,16,128]{3,2,1,0:T(8,128)S(1)} %copy-done.2), custom_call_target="tpu_custom_call" | custom-call | tf_op jit(solution)/shard_map/link/pallas_call | solution.py:461
  (1 shorter events, 0.0 us)
Async XLA Ops:
  0.0 1.0 %copy-start = (f32[2,32,1024]{2,1,0:T(8,128)S(1)}, f32[2,32,1024]{2,1,0:T(8,128)}, u32[]{:S(2)}) copy-start(f32[2,32,1024]{2,1,0:T(8,128)} %param.8) | copy-start | bytes 786436
  0.0 1.6 %copy-start.5 = (f32[2,8,128]{2,1,0:T(8,128)S(1)}, f32[2,8,128]{2,1,0:T(8,128)}, u32[]{:S(2)}) copy-start(f32[2,8,128]{2,1,0:T(8,128)} %constant.18.clone.tw_ref) | copy-start | bytes 24580
  0.0 1.6 %copy-start.3 = (bf16[768,256]{1,0:T(8,128)(2,1)S(1)}, bf16[768,256]{1,0:T(8,128)(2,1)}, u32[]{:S(2)}) copy-start(bf16[768,256]{1,0:T(8,128)(2,1)} %constant.17.clone.bwd_ref) | copy-start | bytes 1179652
  0.0 1.6 %copy-start.4 = (bf16[768,256]{1,0:T(8,128)(2,1)S(1)}, bf16[768,256]{1,0:T(8,128)(2,1)}, u32[]{:S(2)}) copy-start(bf16[768,256]{1,0:T(8,128)(2,1)} %constant.16.clone.fwd_ref) | copy-start | bytes 1179652
  0.0 1.6 %copy-start.1 = (f32[2,8,32,512]{3,2,1,0:T(8,128)S(1)}, f32[2,8,32,512]{3,2,1,0:T(8,128)}, u32[]{:S(2)}) copy-start(f32[2,8,32,512]{3,2,1,0:T(8,128)} %raw_ref.1) | copy-start | bytes 3145732
  1.7 40.8 %copy-start.2 = (f32[2,64,16,128]{3,2,1,0:T(8,128)S(1)}, f32[2,64,16,128]{3,2,1,0:T(8,128)}, u32[]{:S(2)}) copy-start(f32[2,64,16,128]{3,2,1,0:T(8,128)} %s_ref.1) | copy-start | bytes 3145732
